TPU v7x, 512 devices: a whole 4x8x8 slice. The times are simulated.
512 devices in a mesh: ctx: 8 (over y), head: 4 (over x), resp: 16 (over z, core).
Axes of the slice: x: 4, y: 8, z: 8, core: 2. Of those that a mesh axis runs over, the one named last changes fastest.
Arguments:
- prompt_query: bfloat16 [8192, 64, 128], P(('ctx', 'head'), 'resp'), may hold values from -6 to 6
- prompt_key: bfloat16 [8192, 64, 128], P(('ctx', 'head'), 'resp'), may hold values from -6 to 6
- prompt_value: bfloat16 [8192, 64, 128], P(('ctx', 'head'), 'resp'), may hold values from -6 to 6
- prompt_cotangent: bfloat16 [8192, 64, 128], P(('ctx', 'head'), 'resp'), may hold values from -6 to 6
- reply_query: bfloat16 [16, 512, 64, 128], P('resp', None, ('ctx', 'head')), may hold values from -6 to 6
- reply_key: bfloat16 [16, 512, 64, 128], P('resp', None, ('ctx', 'head')), may hold values from -6 to 6
- reply_value: bfloat16 [16, 512, 64, 128], P('resp', None, ('ctx', 'head')), may hold values from -6 to 6
- reply_cotangent: bfloat16 [16, 512, 64, 128], P('resp', None, ('ctx', 'head')), may hold values from -6 to 6
- reply_weight: float32 [16], P('resp'), may hold values from 0.5 to 2
- reply_length: int32 [16], P('resp'), may hold values from 1 to 512, 6144 in all
Outputs:
- prompt_output: bfloat16 [8192, 64, 128], P(('ctx', 'head'), 'resp')
- reply_output: bfloat16 [16, 512, 64, 128], P('resp', None, ('ctx', 'head'))
- prompt_query_grad: bfloat16 [8192, 64, 128], P(('ctx', 'head'), 'resp')
- prompt_key_grad: bfloat16 [8192, 64, 128], P(('ctx', 'head'), 'resp')
- prompt_value_grad: bfloat16 [8192, 64, 128], P(('ctx', 'head'), 'resp')
- reply_query_grad: bfloat16 [16, 512, 64, 128], P('resp', None, ('ctx', 'head'))
- reply_key_grad: bfloat16 [16, 512, 64, 128], P('resp', None, ('ctx', 'head'))
- reply_value_grad: bfloat16 [16, 512, 64, 128], P('resp', None, ('ctx', 'head'))
Inputs may be any that keep to these rules, and one draw needn't show every extreme that they name: `reply_length`: the longest response has exactly 512 live tokens; the slots of a response from its length on are padding.
All inputs are finite; a program needn't handle non-finite values. No bound on the sum of `reply_length` on one device may be relied on, other than what follows from the above.
Results may differ from a plain program's by a relative error of at most 0.0095.
Values sent between devices are 32-bit elements; how exact they have to be, the bound alone decides.
A program may use at most 128 MiB of HBM per device.

v0:
```python
import jax
import jax.numpy as jnp
from jax import lax
from jax.sharding import PartitionSpec as P


def prefix(part, axis, combine, identity, reverse):
    count = lax.axis_size(axis)
    place = lax.axis_index(axis)
    ahead = count - 1 - place if reverse else place
    gathered = lax.all_gather(part, axis)
    state = jnp.zeros_like(part) + jnp.asarray(identity, part.dtype)

    def one(lap, state):
        source = count - 1 - lap if reverse else lap
        return combine(state, lax.dynamic_index_in_dim(gathered, source, 0, False))

    return lax.fori_loop(0, ahead, one, state)


def position_scale(first_row, row_total, head_size):
    positions = (first_row + jnp.arange(row_total, dtype=jnp.int32)).astype(jnp.float32)
    return lax.rsqrt(float(head_size) * (positions + 1.0))


def causal_mask(row_total):
    return jnp.arange(row_total)[:, None] >= jnp.arange(row_total)[None, :]


def split_wide(wide):
    upper = wide.astype(jnp.bfloat16)
    lower = (wide - upper.astype(jnp.float32)).astype(jnp.bfloat16)
    return (upper, lower)


def narrow_first(form, narrow, wide):
    upper, lower = split_wide(wide)
    first = jnp.einsum(form, narrow, upper, preferred_element_type=jnp.float32)
    return first + jnp.einsum(form, narrow, lower, preferred_element_type=jnp.float32)


def wide_first(form, wide, narrow):
    upper, lower = split_wide(wide)
    first = jnp.einsum(form, upper, narrow, preferred_element_type=jnp.float32)
    return first + jnp.einsum(form, lower, narrow, preferred_element_type=jnp.float32)


def forward_pieces(query, key_rows, value_rows, row_scale):
    causal = causal_mask(query.shape[0])
    scores = jnp.einsum("thd,shd->hts", query, key_rows, preferred_element_type=jnp.float32)
    mixing = jnp.where(causal[None], scores * row_scale[None, :, None], 0.0).astype(jnp.bfloat16)
    inner_sum = jnp.einsum("hts,she->the", mixing, value_rows, preferred_element_type=jnp.float32)
    return (mixing, inner_sum)


def carried_term(query, state_in, row_scale):
    product = narrow_first("thd,hde->the", query, state_in)
    return row_scale[:, None, None] * product


def local_state(key_rows, value_rows):
    return jnp.einsum("shd,she->hde", key_rows, value_rows, preferred_element_type=jnp.float32)


def local_moment(query, cotangent, row_scale):
    scaled = query.astype(jnp.float32) * row_scale[:, None, None]
    return wide_first("thd,the->hde", scaled, cotangent)


def backward_pieces(query, key_rows, value_rows, cotangent, mixing, row_scale, state_in, suffix_in):
    causal = causal_mask(query.shape[0])
    grad_mixing = jnp.einsum(
        "the,she->hts", cotangent, value_rows, preferred_element_type=jnp.float32
    )
    grad_scores = jnp.where(causal[None], grad_mixing * row_scale[None, :, None], 0.0).astype(
        jnp.bfloat16
    )
    grad_query = jnp.einsum(
        "hts,shd->thd", grad_scores, key_rows, preferred_element_type=jnp.float32
    )
    grad_query = grad_query + row_scale[:, None, None] * narrow_first(
        "the,hde->thd", cotangent, state_in
    )
    grad_key = jnp.einsum("hts,thd->shd", grad_scores, query, preferred_element_type=jnp.float32)
    grad_value = jnp.einsum("hts,the->she", mixing, cotangent, preferred_element_type=jnp.float32)
    if suffix_in is not None:
        grad_key = grad_key + narrow_first("she,hde->shd", value_rows, suffix_in)
        grad_value = grad_value + narrow_first("shd,hde->she", key_rows, suffix_in)
    return (
        grad_query.astype(jnp.bfloat16),
        grad_key.astype(jnp.bfloat16),
        grad_value.astype(jnp.bfloat16),
    )


def add_states(earlier, later):
    return earlier + later


def shards(
    prompt_query,
    prompt_key,
    prompt_value,
    prompt_cotangent,
    reply_query,
    reply_key,
    reply_value,
    reply_cotangent,
    reply_weight,
    reply_length,
):
    prompt_rows = prompt_query.shape[0]
    prompt_heads = prompt_query.shape[1]
    head_size = prompt_query.shape[2]
    reply_rows = reply_query.shape[1]
    reply_heads = reply_query.shape[2]
    ctx_count = lax.axis_size("ctx")
    head_count = lax.axis_size("head")
    block_index = lax.axis_index("ctx") * head_count + lax.axis_index("head")
    resp_index = lax.axis_index("resp")
    prompt_scale = position_scale(block_index * prompt_rows, prompt_rows, head_size)
    prompt_mixing, prompt_inner = forward_pieces(
        prompt_query, prompt_key, prompt_value, prompt_scale
    )
    prompt_local = local_state(prompt_key, prompt_value)
    zero_state = jnp.zeros_like(prompt_local)
    prompt_before = prefix(prompt_local, ("ctx", "head"), add_states, zero_state, False)
    prompt_total = lax.psum(prompt_local, ("ctx", "head"))
    prompt_output = (prompt_inner + carried_term(prompt_query, prompt_before, prompt_scale)).astype(
        jnp.bfloat16
    )
    reply_first = block_index * reply_heads
    every_state = lax.all_gather(prompt_total, "resp", axis=0, tiled=True)
    reply_state = lax.dynamic_slice_in_dim(every_state, reply_first, reply_heads, 0)
    query_rows = reply_query[0]
    key_rows = reply_key[0]
    value_rows = reply_value[0]
    reply_scale = position_scale(ctx_count * head_count * prompt_rows, reply_rows, head_size)
    live_mask = (jnp.arange(reply_rows, dtype=jnp.int32) < reply_length[0])[:, None, None]
    reply_mixing, reply_inner = forward_pieces(query_rows, key_rows, value_rows, reply_scale)
    reply_output = jnp.where(
        live_mask, reply_inner + carried_term(query_rows, reply_state, reply_scale), 0.0
    ).astype(jnp.bfloat16)
    weighted = (
        reply_weight[0] * jnp.where(live_mask, reply_cotangent[0].astype(jnp.float32), 0.0)
    ).astype(jnp.bfloat16)
    reply_dquery, reply_dkey, reply_dvalue = backward_pieces(
        query_rows, key_rows, value_rows, weighted, reply_mixing, reply_scale, reply_state, None
    )
    reply_local = local_moment(query_rows, weighted, reply_scale)
    moment_sum = lax.psum(reply_local, "resp")
    prompt_first = resp_index * prompt_heads
    every_moment = lax.all_gather(moment_sum, ("ctx", "head"), axis=0, tiled=True)
    prompt_after = lax.dynamic_slice_in_dim(every_moment, prompt_first, prompt_heads, 0)
    prompt_moment = local_moment(prompt_query, prompt_cotangent, prompt_scale)
    later_sum = prefix(prompt_moment, ("ctx", "head"), add_states, zero_state, True)
    suffix = later_sum + prompt_after
    prompt_dquery, prompt_dkey, prompt_dvalue = backward_pieces(
        prompt_query,
        prompt_key,
        prompt_value,
        prompt_cotangent,
        prompt_mixing,
        prompt_scale,
        prompt_before,
        suffix,
    )
    return (
        prompt_output,
        reply_output[None],
        prompt_dquery,
        prompt_dkey,
        prompt_dvalue,
        reply_dquery[None],
        reply_dkey[None],
        reply_dvalue[None],
    )


def solution(mesh):
    placed = (
        P(("ctx", "head"), "resp", None),
        P(("ctx", "head"), "resp", None),
        P(("ctx", "head"), "resp", None),
        P(("ctx", "head"), "resp", None),
        P("resp", None, ("ctx", "head"), None),
        P("resp", None, ("ctx", "head"), None),
        P("resp", None, ("ctx", "head"), None),
        P("resp", None, ("ctx", "head"), None),
        P("resp"),
        P("resp"),
    )
    return jax.shard_map(
        shards,
        mesh=mesh,
        in_specs=placed,
        out_specs=(
            P(("ctx", "head"), "resp", None),
            P("resp", None, ("ctx", "head"), None),
            P(("ctx", "head"), "resp", None),
            P(("ctx", "head"), "resp", None),
            P(("ctx", "head"), "resp", None),
            P("resp", None, ("ctx", "head"), None),
            P("resp", None, ("ctx", "head"), None),
            P("resp", None, ("ctx", "head"), None),
        ),
        check_vma=False,
    )
```

profile of v0, /device:TPU:1, one launch (start us, length us, event | category | flops | bytes accessed | tf_op | source)
XLA Modules:
  0.0 546.7 jit_solution(15241742526547740648)
XLA Ops:
  8.1 2.1 fusion.62
  11.6 1.5 fusion.35
  13.1 1.1 convolution_add_fusion.7
  14.6 105.7 %all-gather.11.cloned.1.call-done = f32[128,128,128]{2,1,0:T(8,128)} async-done(((f32[4,128,128]{2,1,0:T(8,128)}), f32[128,128,128]{2,1,0:T(8,128)}) %all-gather.11.cloned.1.call-update) | async-done | bytes 8388624 | tf_op jit(solution)/shard_map/all_gather | solution.py:11
  121.2 1.0 convolution_add_fusion.6
  122.3 15.0 %all-reduce.5.cloned.1.call-done = f32[2,128,128]{2,1,0:T(8,128)} async-done(((f32[2,128,128]{2,1,0:T(8,128)}), f32[2,128,128]{2,1,0:T(8,128)}) %all-reduce.5.cloned.1.call-update) | async-done | bytes 131088 | tf_op jit(solution)/shard_map/psum | solution.py:151
  137.4 155.6 %all-reduce.3.cloned.1.call-done = f32[4,128,128]{2,1,0:T(8,128)} async-done(((f32[4,128,128]{2,1,0:T(8,128)}), f32[4,128,128]{2,1,0:T(8,128)}) %all-reduce.3.cloned.1.call-update) | async-done | bytes 262160 | tf_op jit(solution)/shard_map/psum | solution.py:128
  297.8 1.1 convolution_bitcast_fusion.3
  298.9 1.1 convolution_bitcast_fusion.2
  300.1 1.1 convolution_bitcast_fusion.5
  301.1 1.2 convolution_bitcast_fusion.1
  302.6 1.3 fusion.22
  306.2 94.3 %all-gather.13.cloned.1.call-done = f32[128,128,128]{2,1,0:T(8,128)} async-done(((f32[4,128,128]{2,1,0:T(8,128)}), f32[128,128,128]{2,1,0:T(8,128)}) %all-gather.13.cloned.1.call-update) | async-done | bytes 8388624 | tf_op jit(solution)/shard_map/all_gather | solution.py:11
  400.5 32.2 %while.23 = (s32[]{:T(128)}, f32[4,128,128]{2,1,0:T(8,128)S(1)}, s32[]{:T(128)}, f32[32,4,128,128]{3,2,1,0:T(8,128)}, s32[]{:T(128)}, /*index=5*/s32[]{:T(128)}, s32[]{:T(128)}, s32[]{:T(128)}) while((s32[]{:T(128)}, f32[4,128,128]{2,1,0:T(8,128)S(1)}, s32[]{:T(128)}, f32[32,4,128,128]{3,2,1,0:T(8,128)}, s32[]{:T(128)}, /*index=5*/s32[]{:T(128)}, ...), condition=%wide.region_4.5_spmd, body=%wide.region_3.4_spmd.sunk | while | flops 65542 | bytes 786575 | solution.py:18
  400.5 1.1 bitcast_add_fusion.5
  401.6 1.0 bitcast_add_fusion.5
  402.6 1.0 bitcast_add_fusion.5
  403.6 1.0 bitcast_add_fusion.5
  404.7 1.0 bitcast_add_fusion.5
  405.7 1.0 bitcast_add_fusion.5
  406.8 1.0 bitcast_add_fusion.5
  407.8 1.0 bitcast_add_fusion.5
  408.8 1.0 bitcast_add_fusion.5
  409.9 1.0 bitcast_add_fusion.5
  410.9 1.0 bitcast_add_fusion.5
  411.9 1.0 bitcast_add_fusion.5
  413.0 1.0 bitcast_add_fusion.5
  414.0 1.0 bitcast_add_fusion.5
  415.0 1.0 bitcast_add_fusion.5
  416.1 1.0 bitcast_add_fusion.5
  417.1 1.0 bitcast_add_fusion.5
  418.2 1.0 bitcast_add_fusion.5
  419.2 1.0 bitcast_add_fusion.5
  420.2 1.0 bitcast_add_fusion.5
  421.3 1.0 bitcast_add_fusion.5
  422.3 1.0 bitcast_add_fusion.5
  423.3 1.0 bitcast_add_fusion.5
  424.4 1.0 bitcast_add_fusion.5
  425.4 1.0 bitcast_add_fusion.5
  426.5 1.0 bitcast_add_fusion.5
  427.5 1.0 bitcast_add_fusion.5
  428.5 1.0 bitcast_add_fusion.5
  429.6 1.0 bitcast_add_fusion.5
  430.6 1.0 bitcast_add_fusion.5
  431.6 1.0 bitcast_add_fusion.5
  432.7 52.9 %all-gather.9.cloned.1.call-done = f32[64,128,128]{2,1,0:T(8,128)} async-done(((f32[2,128,128]{2,1,0:T(8,128)}), f32[64,128,128]{2,1,0:T(8,128)}) %all-gather.9.cloned.1.call-update) | async-done | bytes 4194320 | tf_op jit(solution)/shard_map/all_gather | solution.py:153
  485.6 1.0 subtract_convert_fusion.3
  489.4 44.8 %all-gather.7.cloned.1.call-done = f32[64,128,128]{2,1,0:T(8,128)} async-done(((f32[4,128,128]{2,1,0:T(8,128)}), f32[64,128,128]{2,1,0:T(8,128)}) %all-gather.7.cloned.1.call-update) | async-done | bytes 4194320 | tf_op jit(solution)/shard_map/all_gather | solution.py:133
  (79 shorter events, 16.3 us)
Async XLA Ops:
  8.0 285.2 %copy-start = (bf16[1,512,2,128]{3,2,1,0:T(2,128)(2,1)S(1)}, bf16[1,512,2,128]{3,2,1,0:T(2,128)(2,1)}, u32[]{:S(2)}) copy-start(bf16[1,512,2,128]{3,2,1,0:T(2,128)(2,1)} %param.20) | copy-start | bytes 786436
  8.0 5.1 copy-start.7
  8.0 5.1 copy-start.8
  8.0 6.2 %copy-start.4 = (bf16[256,4,128]{2,1,0:T(4,128)(2,1)S(1)}, bf16[256,4,128]{2,1,0:T(4,128)(2,1)}, u32[]{:S(2)}) copy-start(bf16[256,4,128]{2,1,0:T(4,128)(2,1)} %param.14) | copy-start | bytes 786436
  8.0 112.3 %all-gather.11.cloned.1.call-start = ((), (), s32[]{:S(2)}) async-start(), calls=%async_computation.4 | async-start | bytes 8650752 | tf_op jit(solution)/shard_map/all_gather | solution.py:11
  10.2 110.8 %copy-start.1 = (bf16[256,4,128]{2,1,0:T(4,128)(2,1)S(1)}, bf16[256,4,128]{2,1,0:T(4,128)(2,1)}, u32[]{:S(2)}) copy-start(bf16[256,4,128]{2,1,0:T(4,128)(2,1)} %param.17) | copy-start | bytes 786436
  10.2 127.1 %all-reduce.5.cloned.1.call-start = ((), (), s32[]{:S(2)}) async-start(), calls=%async_computation.2 | async-start | bytes 262144 | tf_op jit(solution)/shard_map/psum | solution.py:151
  120.3 172.7 %all-reduce.3.cloned.1.call-start = ((), (), s32[]{:S(2)}) async-start(), calls=%async_computation | async-start | bytes 524288 | tf_op jit(solution)/shard_map/psum | solution.py:128
  120.9 279.5 %all-gather.13.cloned.1.call-start = ((), (), s32[]{:S(2)}) async-start(), calls=%async_computation.5 | async-start | bytes 8650752 | tf_op jit(solution)/shard_map/all_gather | solution.py:11
  122.3 363.3 %all-gather.9.cloned.1.call-start = ((), (), s32[]{:S(2)}) async-start(), calls=%async_computation.3 | async-start | bytes 4325376 | tf_op jit(solution)/shard_map/all_gather | solution.py:153
  137.3 396.8 %all-gather.7.cloned.1.call-start = ((), (), s32[]{:S(2)}) async-start(), calls=%async_computation.1 | async-start | bytes 4456448 | tf_op jit(solution)/shard_map/all_gather | solution.py:133
  293.2 2.1 copy-start.12
  293.8 1.5 copy-start.5
  295.3 1.9 copy-start.3
  295.8 1.7 copy-start.2
  302.4 2.6 copy-start.9
  400.5 86.4 %copy-start.11 = (f32[256,4,128]{2,0,1:T(8,128)S(1)}, f32[256,4,128]{2,0,1:T(8,128)}, u32[]{:S(2)}) copy-start(f32[256,4,128]{2,0,1:T(8,128)} %convolution_bitcast_fusion.2) | copy-start | bytes 1572868
  486.6 1.6 copy-start.10
  535.7 2.0 copy-start.6
  535.7 2.0 copy-start.13
Sparse Core Ops, SparseCore 0:
  12.6 107.6 all-gather.10
Sparse Core Ops, SparseCore 1:
  14.3 122.9 all-reduce.4
  141.2 151.8 all-reduce.2
  296.7 103.7 all-gather.12
  403.6 81.9 all-gather.8
  487.7 46.4 all-gather.6
where the time goes:
time: 548 us; the launch traced here: 547 us
  waiting for transfers between devices  469 us (86%)
  other arithmetic  33 us (6%)
  matrix products  17.9 us (3%)
  between operations  17.4 us (3%)
  local copies, waits for them, and re-layouts  8.54 us (2%)
    all_gather x2, waiting for transfers between devices, prefix(): gathered = lax.all_gather(part, axis)  200 us
    psum x1, waiting for transfers between devices, shards(): prompt_total = lax.psum(prompt_local, ('ctx', 'head'))  156 us
    all_gather x1, waiting for transfers between devices, shards(): lax.all_gather(moment_sum, ('ctx', 'head'), axis=0, tiled=True)  52.9 us
    all_gather x1, waiting for transfers between devices, shards(): every_state = lax.all_gather(prompt_total, 'resp', axis=0, tiled=True)  44.8 us
    add x31, other arithmetic, add_states(): return earlier + later  31.5 us
    psum x1, waiting for transfers between devices, shards(): moment_sum = lax.psum(reply_local, 'resp')  15 us
  transfers between devices with their start and end apart: 6, of which 6 were waited for; matrix products, arithmetic and copies ran while one was open for 10% of the time, Pallas kernels for 0%

commit v1 on v0

v1 whole, which is shorter than its diff:
```python
import jax
import jax.numpy as jnp
from jax import lax
from jax.experimental import pallas as pl
from jax.experimental.pallas import tpu as pltpu
from jax.sharding import PartitionSpec as P

MESH = pl.DeviceIdType.MESH
F32 = jnp.float32
BF16 = jnp.bfloat16
NY, NX, NZ, NC = 8, 4, 8, 2
E = 128
ROWS = 1024
PROMPT_HEADS = 4
REPLY_HEADS = 2
BLK = 256
SL = E // NY

NN = (((1,), (0,)), ((), ()))
NT = (((1,), (1,)), ((), ()))
TN = (((0,), (0,)), ((), ()))


def dot(a, b, dims):
    return lax.dot_general(a, b, dims, preferred_element_type=F32)


def scale_rows(x, first, heads):
    s = lax.broadcasted_iota(jnp.int32, x.shape, 0)
    pos = (first + s // heads).astype(F32)
    return (x.astype(F32) * lax.rsqrt(float(E) * (pos + 1.0))).astype(BF16)


def by_head(x, heads):
    period = lax.broadcasted_iota(jnp.int32, (16, E), 0) & (heads - 1)
    tiles = x.reshape(ROWS // 16, 16, E)
    parts = []
    for h in range(heads):
        keep = jnp.where(period == h, 1.0, 0.0).astype(BF16)
        parts.append((tiles * keep[None]).reshape(ROWS, E))
    return jnp.concatenate(parts, axis=1)


def reply_weighted(c, weight, length):
    s = lax.broadcasted_iota(jnp.int32, c.shape, 0)
    live = (s // REPLY_HEADS) < length
    return (weight * jnp.where(live, c.astype(F32), 0.0)).astype(BF16)


def wait_bytes(view, sem):
    pltpu.make_async_copy(view, view, sem).wait()


def exchange_kernel(
    pq, pk, pv, pc, rq, rc, weight, length,
    bef_out, aft_out, fin_out,
    loc, wl, xr, yt, yr, ys, yb, xs, st, zf, fin, wr, wz, wzr,
    x_send, x_recv, y_send, y_recv, b_send, b_recv, s_send, s_recv,
    z_send, z_recv, f_send, f_recv, w_send, w_recv, v_send, v_recv,
):
    y = lax.axis_index("ctx")
    x = lax.axis_index("head")
    r = lax.axis_index("resp")
    z = r // 2
    c = r % 2
    fx = 2 * c + x // 2
    wc = x // 2
    wx = 2 * (x % 2)
    loops_back = fx == x

    barrier = pltpu.get_barrier_semaphore()

    def signal(device):
        pl.semaphore_signal(barrier, inc=1, device_id=device, device_id_type=MESH)

    def is_me(device):
        return (device[0] == y) & (device[1] == x) & (device[2] == r)

    def row_peer(d):
        return (y, (x + d) % NX, r)

    def col_peer(d):
        return ((y + d) % NY, x, r)

    def z_peer(d):
        return (y, x, 2 * ((z + d) % NZ) + c)

    def fin_peer(n):
        return (n // 2, fx, 2 * z + n % 2)

    def w_peer(n):
        return (n // 2, wx + n % 2, 2 * z + wc)

    @pl.loop(1, NX)
    def _(d):
        signal(row_peer(d))

    @pl.loop(1, NY)
    def _(d):
        signal(col_peer(d))
        signal(z_peer(d))

    @pl.loop(0, 16)
    def _(n):
        one, two = fin_peer(n), w_peer(n)

        @pl.when(jnp.logical_not(is_me(one)))
        def _():
            signal(one)

        @pl.when(jnp.logical_not(is_me(two)))
        def _():
            signal(two)

    block = y * NX + x
    wide = dot(pk[...], by_head(pv[...], PROMPT_HEADS), TN)
    for h in range(PROMPT_HEADS):
        loc[0, h] = wide[:, h * E:(h + 1) * E]

    @pl.when(loops_back)
    def _():
        pl.semaphore_wait(barrier, 3 + 7 + 7 + 30)

    @pl.when(jnp.logical_not(loops_back))
    def _():
        pl.semaphore_wait(barrier, 3 + 7 + 7 + 32)

    def x_copy(k, d):
        peer = row_peer(d)
        return pltpu.make_async_remote_copy(
            src_ref=loc.at[k, peer[1]], dst_ref=xr.at[k, x],
            send_sem=x_send.at[k], recv_sem=x_recv.at[k],
            device_id=peer, device_id_type=MESH)

    def x_start(k):
        @pl.loop(1, NX)
        def _(d):
            x_copy(k, d).start()
        xr[k, x] = loc[k, x]

    x_start(0)

    weighted = reply_weighted(rc[...], weight[0], length[0])
    rqs = scale_rows(rq[...], NY * NX * (ROWS // PROMPT_HEADS), REPLY_HEADS)
    wide = dot(rqs, by_head(weighted, REPLY_HEADS), TN)
    for i in range(REPLY_HEADS):
        wl[i] = wide[:, i * E:(i + 1) * E].reshape(NY, SL, E)

    @pl.loop(0, 16)
    def _(n):
        peer = w_peer(n)

        @pl.when(jnp.logical_not(is_me(peer)))
        def _():
            pltpu.make_async_remote_copy(
                src_ref=wl.at[n % 2, n // 2], dst_ref=wr.at[2 * y + c],
                send_sem=w_send, recv_sem=w_recv,
                device_id=peer, device_id_type=MESH).start()

    @pl.when(loops_back)
    def _():
        wr[2 * y + c] = wl[x % 2, y]

    pqs = scale_rows(pq[...], block * (ROWS // PROMPT_HEADS), PROMPT_HEADS)
    wide = dot(pqs, by_head(pc[...], PROMPT_HEADS), TN)
    for h in range(PROMPT_HEADS):
        loc[1, h] = wide[:, h * E:(h + 1) * E]
    x_start(1)

    def y_start(k):
        wait_bytes(xr.at[k, pl.ds(0, NX - 1)], x_recv.at[k])
        total = (xr[k, 0] + xr[k, 1]) + (xr[k, 2] + xr[k, 3])
        yt[k] = total.reshape(NY, SL, E)

        @pl.loop(1, NY)
        def _(d):
            peer = col_peer(d)
            pltpu.make_async_remote_copy(
                src_ref=yt.at[k, peer[0]], dst_ref=yr.at[k, y],
                send_sem=y_send.at[k], recv_sem=y_recv.at[k],
                device_id=peer, device_id_type=MESH).start()
        yr[k, y] = yt[k, y]

    def b_start(k):
        @pl.loop(1, NY)
        def _(d):
            peer = col_peer(d)
            pltpu.make_async_remote_copy(
                src_ref=ys.at[k, peer[0]], dst_ref=yb.at[k, y],
                send_sem=b_send.at[k], recv_sem=b_recv.at[k],
                device_id=peer, device_id_type=MESH).start()
        yb[k, y] = ys[k, y]

    def s_start(k):
        @pl.loop(1, NX)
        def _(d):
            peer = row_peer(d)
            pltpu.make_async_remote_copy(
                src_ref=xs.at[k, peer[1]], dst_ref=st.at[k, x],
                send_sem=s_send.at[k], recv_sem=s_recv.at[k],
                device_id=peer, device_id_type=MESH).start()
        st[k, x] = xs[k, x]

    y_start(0)

    @pl.when(loops_back)
    def _():
        wait_bytes(wr.at[pl.ds(0, 15)], w_recv)

    @pl.when(jnp.logical_not(loops_back))
    def _():
        wait_bytes(wr, w_recv)

    for n in range(NY):
        wz[n] = wr[2 * n] + wr[2 * n + 1]

    @pl.loop(1, NZ)
    def _(d):
        to = (z + d) % NZ
        pltpu.make_async_remote_copy(
            src_ref=wz.at[to], dst_ref=wzr.at[z],
            send_sem=v_send, recv_sem=v_recv,
            device_id=(y, x, 2 * to + c), device_id_type=MESH).start()
    wzr[z] = wz[z]

    wait_bytes(yr.at[0, pl.ds(0, NY - 1)], y_recv.at[0])
    running = jnp.zeros((SL, E), F32)
    for n in range(NY):
        ys[0, n] = running
        running = running + yr[0, n]
    zf[z] = running
    b_start(0)

    @pl.loop(1, NZ)
    def _(d):
        pltpu.make_async_remote_copy(
            src_ref=zf.at[z], dst_ref=zf.at[z],
            send_sem=z_send, recv_sem=z_recv,
            device_id=z_peer(d), device_id_type=MESH).start()

    y_start(1)

    wait_bytes(yb.at[0, pl.ds(0, NY - 1)], b_recv.at[0])
    running = yb[0].reshape(E, E)
    for n in range(NX):
        xs[0, n] = running
        if n < NX - 1:
            running = running + xr[0, n]
    s_start(0)

    wait_bytes(wzr.at[pl.ds(0, NZ - 1)], v_recv)
    wait_bytes(yr.at[1, pl.ds(0, NY - 1)], y_recv.at[1])
    running = wzr[0]
    for n in range(1, NZ):
        running = running + wzr[n]
    for n in reversed(range(NY)):
        ys[1, n] = running
        if n > 0:
            running = running + yr[1, n]
    b_start(1)

    wait_bytes(zf.at[pl.ds(0, NZ - 1)], z_recv)

    @pl.loop(0, 16)
    def _(n):
        peer = fin_peer(n)

        @pl.when(jnp.logical_not(is_me(peer)))
        def _():
            pltpu.make_async_remote_copy(
                src_ref=zf.at[n // 2], dst_ref=fin.at[(x % 2) * NY + y],
                send_sem=f_send, recv_sem=f_recv,
                device_id=peer, device_id_type=MESH).start()

    @pl.when(loops_back)
    def _():
        fin[(x % 2) * NY + y] = zf[y]

    wait_bytes(yb.at[1, pl.ds(0, NY - 1)], b_recv.at[1])
    running = yb[1].reshape(E, E)
    for n in reversed(range(NX)):
        xs[1, n] = running
        if n > 0:
            running = running + xr[1, n]
    s_start(1)

    wait_bytes(st.at[0, pl.ds(0, NX - 1)], s_recv.at[0])
    bef_out[...] = st[0].reshape(NX * E, E).astype(BF16)

    @pl.when(loops_back)
    def _():
        wait_bytes(fin.at[pl.ds(0, 15)], f_recv)

    @pl.when(jnp.logical_not(loops_back))
    def _():
        wait_bytes(fin, f_recv)

    fin_out[...] = fin[...].reshape(REPLY_HEADS * E, E).astype(BF16)
    wait_bytes(st.at[1, pl.ds(0, NX - 1)], s_recv.at[1])
    aft_out[...] = st[1].reshape(NX * E, E).astype(BF16)

    for k in range(2):
        wait_bytes(loc.at[k, pl.ds(0, NX - 1)], x_send.at[k])
        wait_bytes(yt.at[k, pl.ds(0, NY - 1)], y_send.at[k])
        wait_bytes(ys.at[k, pl.ds(0, NY - 1)], b_send.at[k])
        wait_bytes(xs.at[k, pl.ds(0, NX - 1)], s_send.at[k])
    wait_bytes(zf.at[pl.ds(0, NZ - 1)], z_send)
    wait_bytes(wz.at[pl.ds(0, NZ - 1)], v_send)

    @pl.when(loops_back)
    def _():
        wait_bytes(fin.at[pl.ds(0, 15)], f_send)
        wait_bytes(wr.at[pl.ds(0, 15)], w_send)

    @pl.when(jnp.logical_not(loops_back))
    def _():
        wait_bytes(fin, f_send)
        wait_bytes(wr, w_send)


def exchange(pq, pk, pv, pc, rq, rc, weight, length):
    vmem = pl.BlockSpec(memory_space=pltpu.VMEM)
    smem = pl.BlockSpec(memory_space=pltpu.SMEM)
    dma = pltpu.SemaphoreType.DMA
    state = (E, E)
    return pl.pallas_call(
        exchange_kernel,
        out_shape=(
            jax.ShapeDtypeStruct((PROMPT_HEADS * E, E), BF16),
            jax.ShapeDtypeStruct((PROMPT_HEADS * E, E), BF16),
            jax.ShapeDtypeStruct((REPLY_HEADS * E, E), BF16),
        ),
        in_specs=[vmem] * 6 + [smem] * 2,
        out_specs=(vmem, vmem, vmem),
        scratch_shapes=[
            pltpu.VMEM((2, NX) + state, F32),
            pltpu.VMEM((2, NY, SL, E), F32),
            pltpu.VMEM((2, NX) + state, F32),
            pltpu.VMEM((2, NY, SL, E), F32),
            pltpu.VMEM((2, NY, SL, E), F32),
            pltpu.VMEM((2, NY, SL, E), F32),
            pltpu.VMEM((2, NY, SL, E), F32),
            pltpu.VMEM((2, NX) + state, F32),
            pltpu.VMEM((2, NX) + state, F32),
            pltpu.VMEM((NZ, SL, E), F32),
            pltpu.VMEM((16, SL, E), F32),
            pltpu.VMEM((16, SL, E), F32),
            pltpu.VMEM((NZ, SL, E), F32),
            pltpu.VMEM((NZ, SL, E), F32),
            dma((2,)), dma((2,)), dma((2,)), dma((2,)),
            dma((2,)), dma((2,)), dma((2,)), dma((2,)),
            dma, dma, dma, dma, dma, dma, dma, dma,
        ],
        compiler_params=pltpu.CompilerParams(
            collective_id=0, has_side_effects=True),
        name="exchange",
    )(pq, pk, pv, pc, rq, rc, weight, length)


def pair_masks(heads):
    a = lax.broadcasted_iota(jnp.int32, (BLK, BLK), 0)
    b = lax.broadcasted_iota(jnp.int32, (BLK, BLK), 1)
    same = ((a ^ b) & (heads - 1)) == 0
    off = jnp.where(same, 1.0, 0.0)
    diag = jnp.where(a >= b, off, 0.0)
    return off.astype(BF16), diag.astype(BF16)


def mixings(left, right, heads, dest):
    off, diag = pair_masks(heads)
    for i in range(ROWS // BLK):
        rows = pl.ds(i * BLK, BLK)
        for j in range(i + 1):
            cols = pl.ds(j * BLK, BLK)
            part = dot(left[i * BLK:(i + 1) * BLK], right[j * BLK:(j + 1) * BLK], NT)
            dest[rows, cols] = part.astype(BF16) * (diag if i == j else off)


def finish_kernel(
    pq, pk, pv, pc, rq, rk, rv, rc, bef, aft, fin, weight, length,
    po, pdq, pdk, pdv, ro, rdq, rdk, rdv,
    mix, gmix, lin,
):
    block = lax.axis_index("ctx") * NX + lax.axis_index("head")

    def blocks(narrow, wide_out, grad_out, key_out, value_out, q, k, v, cot, live):
        for i in range(ROWS // BLK):
            rows = slice(i * BLK, (i + 1) * BLK)
            upto = slice(0, (i + 1) * BLK)
            onward = slice(i * BLK, ROWS)
            part = dot(mix[rows, upto], v[upto], NN) + lin[0, rows]
            if live is not None:
                s = i * BLK + lax.broadcasted_iota(jnp.int32, (BLK, E), 0)
                part = jnp.where((s // REPLY_HEADS) < live, part, 0.0)
            wide_out[rows] = part.astype(BF16)
            part = dot(gmix[rows, upto], k[upto], NN) + lin[1, rows]
            grad_out[rows] = part.astype(BF16)
            part = dot(gmix[onward, rows], q[onward], TN)
            if narrow:
                part = part + lin[2, rows]
            key_out[rows] = part.astype(BF16)
            part = dot(mix[onward, rows], cot[onward], TN)
            if narrow:
                part = part + lin[3, rows]
            value_out[rows] = part.astype(BF16)

    first = block * (ROWS // PROMPT_HEADS)
    qs = scale_rows(pq[...], first, PROMPT_HEADS)
    cs = scale_rows(pc[...], first, PROMPT_HEADS)
    before = bef[...]
    before_wide = jnp.concatenate(
        [before[h * E:(h + 1) * E] for h in range(PROMPT_HEADS)], axis=1)
    after = aft[...]
    after_wide = jnp.concatenate(
        [after[h * E:(h + 1) * E] for h in range(PROMPT_HEADS)], axis=1)
    lin[0] = dot(by_head(qs, PROMPT_HEADS), before, NN)
    lin[1] = dot(by_head(cs, PROMPT_HEADS), before_wide, NT)
    lin[2] = dot(by_head(pv[...], PROMPT_HEADS), after_wide, NT)
    lin[3] = dot(by_head(pk[...], PROMPT_HEADS), after, NN)
    mixings(qs, pk[...], PROMPT_HEADS, mix)
    mixings(cs, pv[...], PROMPT_HEADS, gmix)
    blocks(True, po, pdq, pdk, pdv, pq, pk, pv, pc, None)

    weighted = reply_weighted(rc[...], weight[0], length[0])
    first = NY * NX * (ROWS // PROMPT_HEADS)
    qs = scale_rows(rq[...], first, REPLY_HEADS)
    cs = scale_rows(weighted, first, REPLY_HEADS)
    final = fin[...]
    final_wide = jnp.concatenate(
        [final[h * E:(h + 1) * E] for h in range(REPLY_HEADS)], axis=1)
    lin[0] = dot(by_head(qs, REPLY_HEADS), final, NN)
    lin[1] = dot(by_head(cs, REPLY_HEADS), final_wide, NT)
    mixings(qs, rk[...], REPLY_HEADS, mix)
    mixings(cs, rv[...], REPLY_HEADS, gmix)
    blocks(False, ro, rdq, rdk, rdv, rq, rk, rv, weighted, length[0])


def finish(pq, pk, pv, pc, rq, rk, rv, rc, bef, aft, fin, weight, length):
    vmem = pl.BlockSpec(memory_space=pltpu.VMEM)
    smem = pl.BlockSpec(memory_space=pltpu.SMEM)
    return pl.pallas_call(
        finish_kernel,
        out_shape=tuple([jax.ShapeDtypeStruct((ROWS, E), BF16)] * 8),
        in_specs=[vmem] * 11 + [smem] * 2,
        out_specs=tuple([vmem] * 8),
        scratch_shapes=[
            pltpu.VMEM((ROWS, ROWS), BF16),
            pltpu.VMEM((ROWS, ROWS), BF16),
            pltpu.VMEM((4, ROWS, E), F32),
        ],
        name="finish",
    )(pq, pk, pv, pc, rq, rk, rv, rc, bef, aft, fin, weight, length)


def shards(
    prompt_query, prompt_key, prompt_value, prompt_cotangent,
    reply_query, reply_key, reply_value, reply_cotangent,
    reply_weight, reply_length,
):
    prompt_shape = prompt_query.shape
    reply_shape = reply_query.shape
    pq, pk, pv, pc, rq, rk, rv, rc = [
        a.reshape(ROWS, E)
        for a in (prompt_query, prompt_key, prompt_value, prompt_cotangent,
                  reply_query, reply_key, reply_value, reply_cotangent)
    ]
    bef, aft, fin = exchange(pq, pk, pv, pc, rq, rc, reply_weight, reply_length)
    po, pdq, pdk, pdv, ro, rdq, rdk, rdv = finish(
        pq, pk, pv, pc, rq, rk, rv, rc, bef, aft, fin, reply_weight, reply_length)
    return (
        po.reshape(prompt_shape), ro.reshape(reply_shape),
        pdq.reshape(prompt_shape), pdk.reshape(prompt_shape), pdv.reshape(prompt_shape),
        rdq.reshape(reply_shape), rdk.reshape(reply_shape), rdv.reshape(reply_shape),
    )


def solution(mesh):
    prompt = P(("ctx", "head"), "resp", None)
    reply = P("resp", None, ("ctx", "head"), None)
    placed = (prompt,) * 4 + (reply,) * 4 + (P("resp"), P("resp"))
    return jax.shard_map(
        shards,
        mesh=mesh,
        in_specs=placed,
        out_specs=(prompt, reply, prompt, prompt, prompt, reply, reply, reply),
        check_vma=False,
    )
```

time: 548 us -> 53.8 us (0.10)
  the two profiles are of different devices: /device:TPU:1 before, /device:TPU:64 now
where the time goes in v1:
time: 53.8 us; the launch traced here: 53.6 us
  Pallas kernels  51.7 us (96%)
  between operations  1.93 us (4%)
    pallas_call x1, Pallas kernels, exchange(): pl.pallas_call(exchange_kernel, out_shape=(jax.ShapeDtypeStruct((PROMPT_H...  43.5 us
    pallas_call x1, Pallas kernels, finish(): pl.pallas_call(finish_kernel, out_shape=tuple([jax.ShapeDtypeStruct((ROWS...  8.16 us

profile of v1, /device:TPU:64, one launch (start us, length us, event | category | flops | bytes accessed | tf_op | source)
XLA Modules:
  0.0 53.6 jit_solution(3279999369371874873)
XLA Ops:
  1.9 43.5 %exchange.1 = (bf16[512,128]{1,0:T(8,128)(2,1)}, bf16[512,128]{1,0:T(8,128)(2,1)}, bf16[256,128]{1,0:T(8,128)(2,1)}) custom-call(bf16[1024,128]{1,0:T(8,128)(2,1)} %bitcast.16, bf16[1024,128]{1,0:T(8,128)(2,1)} %bitcast.18, bf16[1024,128]{1,0:T(8,128)(2,1)} %bitcast.20, bf16[1024,128]{1,0:T(8,128)(2,1)} %bitcast.22, bf16[1024,128]{1,0:T(8,128)(2,1)} %bitcast.24, ...), custom_call_target="tpu_custom_call" | custom-call | tf_op jit(solution)/shard_map/exchange/pallas_call | solution.py:326
  45.5 8.2 %finish.1 = (bf16[1024,128]{1,0:T(8,128)(2,1)}, bf16[1024,128]{1,0:T(8,128)(2,1)}, bf16[1024,128]{1,0:T(8,128)(2,1)}, bf16[1024,128]{1,0:T(8,128)(2,1)}, bf16[10...) custom-call(bf16[1024,128]{1,0:T(8,128)(2,1)} %bitcast.17, ...), custom_call_target="tpu_custom_call" | custom-call | tf_op jit(solution)/shard_map/finish/pallas_call | solution.py:441

commit v2 on v1

--- a/solution.py
+++ b/solution.py
@@ -51,10 +51,37 @@
     pltpu.make_async_copy(view, view, sem).wait()
 
 
+def pair_masks(heads):
+    a = lax.broadcasted_iota(jnp.int32, (BLK, BLK), 0)
+    b = lax.broadcasted_iota(jnp.int32, (BLK, BLK), 1)
+    same = ((a ^ b) & (heads - 1)) == 0
+    off = jnp.where(same, 1.0, 0.0)
+    diag = jnp.where(a >= b, off, 0.0)
+    return off.astype(BF16), diag.astype(BF16)
+
+
+def mixings(left, right, heads, dest):
+    off, diag = pair_masks(heads)
+    for i in range(ROWS // BLK):
+        rows = pl.ds(i * BLK, BLK)
+        for j in range(i + 1):
+            cols = pl.ds(j * BLK, BLK)
+            part = dot(left[i * BLK:(i + 1) * BLK], right[j * BLK:(j + 1) * BLK], NT)
+            dest[rows, cols] = part.astype(BF16) * (diag if i == j else off)
+
+
+def stack_wide(state, heads):
+    return jnp.concatenate([state[h * E:(h + 1) * E] for h in range(heads)], axis=1)
+
+
 def exchange_kernel(
-    pq, pk, pv, pc, rq, rc, weight, length,
-    bef_out, aft_out, fin_out,
+    pq_in, pk_in, pv_in, pc_in, rq_in, rk_in, rv_in, rc_in, weight, length,
+    po_out, ro_out, pdq_out, rdq_out, rdk_out, rdv_out, pdk_out, pdv_out, aft_out,
+    pq, pk, pv, pc, rq, rk, rv, rc,
+    po, ro, pdq, rdq, rdk, rdv, pdk, pdv, aft,
+    pqs, pcs, rqs, rcs, rw, mix, gmix, part,
     loc, wl, xr, yt, yr, ys, yb, xs, st, zf, fin, wr, wz, wzr,
+    in_sem, out_sem,
     x_send, x_recv, y_send, y_recv, b_send, b_recv, s_send, s_recv,
     z_send, z_recv, f_send, f_recv, w_send, w_recv, v_send, v_recv,
 ):
@@ -70,6 +97,20 @@
 
     barrier = pltpu.get_barrier_semaphore()
 
+    loads = [
+        pltpu.make_async_copy(src, dst, in_sem.at[n])
+        for n, (src, dst) in enumerate((
+            (pk_in, pk), (pv_in, pv), (rq_in, rq), (rc_in, rc),
+            (pq_in, pq), (pc_in, pc), (rk_in, rk), (rv_in, rv)))
+    ]
+    for load in loads:
+        load.start()
+
+    def save(n, src, dst):
+        copy = pltpu.make_async_copy(src, dst, out_sem.at[n])
+        copy.start()
+        return copy
+
     def signal(device):
         pl.semaphore_signal(barrier, inc=1, device_id=device, device_id_type=MESH)
 
@@ -113,6 +154,10 @@
             signal(two)
 
     block = y * NX + x
+    prompt_first = block * (ROWS // PROMPT_HEADS)
+    reply_first = NY * NX * (ROWS // PROMPT_HEADS)
+    loads[0].wait()
+    loads[1].wait()
     wide = dot(pk[...], by_head(pv[...], PROMPT_HEADS), TN)
     for h in range(PROMPT_HEADS):
         loc[0, h] = wide[:, h * E:(h + 1) * E]
@@ -125,24 +170,23 @@
     def _():
         pl.semaphore_wait(barrier, 3 + 7 + 7 + 32)
 
-    def x_copy(k, d):
-        peer = row_peer(d)
-        return pltpu.make_async_remote_copy(
-            src_ref=loc.at[k, peer[1]], dst_ref=xr.at[k, x],
-            send_sem=x_send.at[k], recv_sem=x_recv.at[k],
-            device_id=peer, device_id_type=MESH)
-
     def x_start(k):
         @pl.loop(1, NX)
         def _(d):
-            x_copy(k, d).start()
+            peer = row_peer(d)
+            pltpu.make_async_remote_copy(
+                src_ref=loc.at[k, peer[1]], dst_ref=xr.at[k, x],
+                send_sem=x_send.at[k], recv_sem=x_recv.at[k],
+                device_id=peer, device_id_type=MESH).start()
         xr[k, x] = loc[k, x]
 
     x_start(0)
 
-    weighted = reply_weighted(rc[...], weight[0], length[0])
-    rqs = scale_rows(rq[...], NY * NX * (ROWS // PROMPT_HEADS), REPLY_HEADS)
-    wide = dot(rqs, by_head(weighted, REPLY_HEADS), TN)
+    loads[2].wait()
+    loads[3].wait()
+    rw[...] = reply_weighted(rc[...], weight[0], length[0])
+    rqs[...] = scale_rows(rq[...], reply_first, REPLY_HEADS)
+    wide = dot(rqs[...], by_head(rw[...], REPLY_HEADS), TN)
     for i in range(REPLY_HEADS):
         wl[i] = wide[:, i * E:(i + 1) * E].reshape(NY, SL, E)
 
@@ -161,8 +205,10 @@
     def _():
         wr[2 * y + c] = wl[x % 2, y]
 
-    pqs = scale_rows(pq[...], block * (ROWS // PROMPT_HEADS), PROMPT_HEADS)
-    wide = dot(pqs, by_head(pc[...], PROMPT_HEADS), TN)
+    loads[4].wait()
+    loads[5].wait()
+    pqs[...] = scale_rows(pq[...], prompt_first, PROMPT_HEADS)
+    wide = dot(pqs[...], by_head(pc[...], PROMPT_HEADS), TN)
     for h in range(PROMPT_HEADS):
         loc[1, h] = wide[:, h * E:(h + 1) * E]
     x_start(1)
@@ -201,6 +247,13 @@
                 device_id=peer, device_id_type=MESH).start()
         st[k, x] = xs[k, x]
 
+    blocks = [(slice(i * BLK, (i + 1) * BLK), slice(0, (i + 1) * BLK), slice(i * BLK, ROWS))
+              for i in range(ROWS // BLK)]
+
+    pcs[...] = scale_rows(pc[...], prompt_first, PROMPT_HEADS)
+    mixings(pqs, pk, PROMPT_HEADS, mix)
+    mixings(pcs, pv, PROMPT_HEADS, gmix)
+
     y_start(0)
 
     @pl.when(loops_back)
@@ -223,6 +276,13 @@
             device_id=(y, x, 2 * to + c), device_id_type=MESH).start()
     wzr[z] = wz[z]
 
+    for rows, upto, onward in blocks:
+        pdk[rows] = dot(gmix[onward, rows], pq[onward], TN)
+        pdv[rows] = dot(mix[onward, rows], pc[onward], TN)
+    saves = [save(0, pdk, pdk_out), save(1, pdv, pdv_out)]
+
+    y_start(1)
+
     wait_bytes(yr.at[0, pl.ds(0, NY - 1)], y_recv.at[0])
     running = jnp.zeros((SL, E), F32)
     for n in range(NY):
@@ -238,15 +298,12 @@
             send_sem=z_send, recv_sem=z_recv,
             device_id=z_peer(d), device_id_type=MESH).start()
 
-    y_start(1)
-
-    wait_bytes(yb.at[0, pl.ds(0, NY - 1)], b_recv.at[0])
-    running = yb[0].reshape(E, E)
-    for n in range(NX):
-        xs[0, n] = running
-        if n < NX - 1:
-            running = running + xr[0, n]
-    s_start(0)
+    for rows, upto, onward in blocks:
+        part[0, rows] = dot(mix[rows, upto], pv[upto], NN)
+        part[1, rows] = dot(gmix[rows, upto], pk[upto], NN)
+    loads[6].wait()
+    loads[7].wait()
+    mixings(rqs, rk, REPLY_HEADS, mix)
 
     wait_bytes(wzr.at[pl.ds(0, NZ - 1)], v_recv)
     wait_bytes(yr.at[1, pl.ds(0, NY - 1)], y_recv.at[1])
@@ -276,6 +333,20 @@
     def _():
         fin[(x % 2) * NY + y] = zf[y]
 
+    wait_bytes(yb.at[0, pl.ds(0, NY - 1)], b_recv.at[0])
+    running = yb[0].reshape(E, E)
+    for n in range(NX):
+        xs[0, n] = running
+        if n < NX - 1:
+            running = running + xr[0, n]
+    s_start(0)
+
+    rcs[...] = scale_rows(rw[...], reply_first, REPLY_HEADS)
+    mixings(rcs, rv, REPLY_HEADS, gmix)
+    for rows, upto, onward in blocks:
+        rdv[rows] = dot(mix[onward, rows], rw[onward], TN).astype(BF16)
+    saves.append(save(2, rdv, rdv_out))
+
     wait_bytes(yb.at[1, pl.ds(0, NY - 1)], b_recv.at[1])
     running = yb[1].reshape(E, E)
     for n in reversed(range(NX)):
@@ -284,8 +355,20 @@
             running = running + xr[1, n]
     s_start(1)
 
+    for rows, upto, onward in blocks:
+        rdk[rows] = dot(gmix[onward, rows], rq[onward], TN).astype(BF16)
+    saves.append(save(3, rdk, rdk_out))
+    for rows, upto, onward in blocks:
+        part[2, rows] = dot(mix[rows, upto], rv[upto], NN)
+        part[3, rows] = dot(gmix[rows, upto], rk[upto], NN)
+
     wait_bytes(st.at[0, pl.ds(0, NX - 1)], s_recv.at[0])
-    bef_out[...] = st[0].reshape(NX * E, E).astype(BF16)
+    before = st[0].reshape(NX * E, E).astype(BF16)
+    po[...] = (part[0] + dot(by_head(pqs[...], PROMPT_HEADS), before, NN)).astype(BF16)
+    saves.append(save(4, po, po_out))
+    wide = stack_wide(before, PROMPT_HEADS)
+    pdq[...] = (part[1] + dot(by_head(pcs[...], PROMPT_HEADS), wide, NT)).astype(BF16)
+    saves.append(save(5, pdq, pdq_out))
 
     @pl.when(loops_back)
     def _():
@@ -295,9 +378,18 @@
     def _():
         wait_bytes(fin, f_recv)
 
-    fin_out[...] = fin[...].reshape(REPLY_HEADS * E, E).astype(BF16)
+    final = fin[...].reshape(REPLY_HEADS * E, E).astype(BF16)
+    out = part[2] + dot(by_head(rqs[...], REPLY_HEADS), final, NN)
+    s = lax.broadcasted_iota(jnp.int32, (ROWS, E), 0)
+    ro[...] = jnp.where((s // REPLY_HEADS) < length[0], out, 0.0).astype(BF16)
+    saves.append(save(6, ro, ro_out))
+    wide = stack_wide(final, REPLY_HEADS)
+    rdq[...] = (part[3] + dot(by_head(rcs[...], REPLY_HEADS), wide, NT)).astype(BF16)
+    saves.append(save(7, rdq, rdq_out))
+
     wait_bytes(st.at[1, pl.ds(0, NX - 1)], s_recv.at[1])
-    aft_out[...] = st[1].reshape(NX * E, E).astype(BF16)
+    aft[...] = st[1].reshape(NX * E, E).astype(BF16)
+    saves.append(save(8, aft, aft_out))
 
     for k in range(2):
         wait_bytes(loc.at[k, pl.ds(0, NX - 1)], x_send.at[k])
@@ -317,29 +409,36 @@
         wait_bytes(fin, f_send)
         wait_bytes(wr, w_send)
 
-
-def exchange(pq, pk, pv, pc, rq, rc, weight, length):
-    vmem = pl.BlockSpec(memory_space=pltpu.VMEM)
+    for copy in saves:
+        copy.wait()
+
+
+def exchange(*args):
+    whole = pl.BlockSpec(memory_space=pl.ANY)
     smem = pl.BlockSpec(memory_space=pltpu.SMEM)
     dma = pltpu.SemaphoreType.DMA
     state = (E, E)
+    narrow = pltpu.VMEM((ROWS, E), BF16)
+    wide = pltpu.VMEM((ROWS, E), F32)
+    slices = pltpu.VMEM((2, NY, SL, E), F32)
     return pl.pallas_call(
         exchange_kernel,
-        out_shape=(
-            jax.ShapeDtypeStruct((PROMPT_HEADS * E, E), BF16),
-            jax.ShapeDtypeStruct((PROMPT_HEADS * E, E), BF16),
-            jax.ShapeDtypeStruct((REPLY_HEADS * E, E), BF16),
-        ),
-        in_specs=[vmem] * 6 + [smem] * 2,
-        out_specs=(vmem, vmem, vmem),
-        scratch_shapes=[
+        out_shape=tuple(
+            [jax.ShapeDtypeStruct((ROWS, E), BF16)] * 6
+            + [jax.ShapeDtypeStruct((ROWS, E), F32)] * 2
+            + [jax.ShapeDtypeStruct((PROMPT_HEADS * E, E), BF16)]),
+        in_specs=[whole] * 8 + [smem] * 2,
+        out_specs=tuple([whole] * 9),
+        scratch_shapes=[narrow] * 14 + [wide] * 2 + [
+            pltpu.VMEM((PROMPT_HEADS * E, E), BF16),
+        ] + [narrow] * 5 + [
+            pltpu.VMEM((ROWS, ROWS), BF16),
+            pltpu.VMEM((ROWS, ROWS), BF16),
+            pltpu.VMEM((4, ROWS, E), F32),
             pltpu.VMEM((2, NX) + state, F32),
-            pltpu.VMEM((2, NY, SL, E), F32),
+            slices,
             pltpu.VMEM((2, NX) + state, F32),
-            pltpu.VMEM((2, NY, SL, E), F32),
-            pltpu.VMEM((2, NY, SL, E), F32),
-            pltpu.VMEM((2, NY, SL, E), F32),
-            pltpu.VMEM((2, NY, SL, E), F32),
+            slices, slices, slices, slices,
             pltpu.VMEM((2, NX) + state, F32),
             pltpu.VMEM((2, NX) + state, F32),
             pltpu.VMEM((NZ, SL, E), F32),
@@ -347,6 +446,7 @@
             pltpu.VMEM((16, SL, E), F32),
             pltpu.VMEM((NZ, SL, E), F32),
             pltpu.VMEM((NZ, SL, E), F32),
+            dma((8,)), dma((9,)),
             dma((2,)), dma((2,)), dma((2,)), dma((2,)),
             dma((2,)), dma((2,)), dma((2,)), dma((2,)),
             dma, dma, dma, dma, dma, dma, dma, dma,
@@ -354,102 +454,61 @@
         compiler_params=pltpu.CompilerParams(
             collective_id=0, has_side_effects=True),
         name="exchange",
-    )(pq, pk, pv, pc, rq, rc, weight, length)
-
-
-def pair_masks(heads):
-    a = lax.broadcasted_iota(jnp.int32, (BLK, BLK), 0)
-    b = lax.broadcasted_iota(jnp.int32, (BLK, BLK), 1)
-    same = ((a ^ b) & (heads - 1)) == 0
-    off = jnp.where(same, 1.0, 0.0)
-    diag = jnp.where(a >= b, off, 0.0)
-    return off.astype(BF16), diag.astype(BF16)
-
-
-def mixings(left, right, heads, dest):
-    off, diag = pair_masks(heads)
-    for i in range(ROWS // BLK):
-        rows = pl.ds(i * BLK, BLK)
-        for j in range(i + 1):
-            cols = pl.ds(j * BLK, BLK)
-            part = dot(left[i * BLK:(i + 1) * BLK], right[j * BLK:(j + 1) * BLK], NT)
-            dest[rows, cols] = part.astype(BF16) * (diag if i == j else off)
+    )(*args)
 
 
 def finish_kernel(
-    pq, pk, pv, pc, rq, rk, rv, rc, bef, aft, fin, weight, length,
-    po, pdq, pdk, pdv, ro, rdq, rdk, rdv,
-    mix, gmix, lin,
+    po_in, ro_in, pdq_in, rdq_in, rdk_in, rdv_in, pdk_in, pdv_in, aft_in, pk_in, pv_in,
+    po_out, ro_out, pdq_out, rdq_out, rdk_out, rdv_out, pdk_out, pdv_out,
+    po, ro, pdq, rdq, rdk, rdv, kpart, vpart, aft, pk, pv, pdk, pdv, in_sem, out_sem,
 ):
-    block = lax.axis_index("ctx") * NX + lax.axis_index("head")
-
-    def blocks(narrow, wide_out, grad_out, key_out, value_out, q, k, v, cot, live):
-        for i in range(ROWS // BLK):
-            rows = slice(i * BLK, (i + 1) * BLK)
-            upto = slice(0, (i + 1) * BLK)
-            onward = slice(i * BLK, ROWS)
-            part = dot(mix[rows, upto], v[upto], NN) + lin[0, rows]
-            if live is not None:
-                s = i * BLK + lax.broadcasted_iota(jnp.int32, (BLK, E), 0)
-                part = jnp.where((s // REPLY_HEADS) < live, part, 0.0)
-            wide_out[rows] = part.astype(BF16)
-            part = dot(gmix[rows, upto], k[upto], NN) + lin[1, rows]
-            grad_out[rows] = part.astype(BF16)
-            part = dot(gmix[onward, rows], q[onward], TN)
-            if narrow:
-                part = part + lin[2, rows]
-            key_out[rows] = part.astype(BF16)
-            part = dot(mix[onward, rows], cot[onward], TN)
-            if narrow:
-                part = part + lin[3, rows]
-            value_out[rows] = part.astype(BF16)
-
-    first = block * (ROWS // PROMPT_HEADS)
-    qs = scale_rows(pq[...], first, PROMPT_HEADS)
-    cs = scale_rows(pc[...], first, PROMPT_HEADS)
-    before = bef[...]
-    before_wide = jnp.concatenate(
-        [before[h * E:(h + 1) * E] for h in range(PROMPT_HEADS)], axis=1)
-    after = aft[...]
-    after_wide = jnp.concatenate(
-        [after[h * E:(h + 1) * E] for h in range(PROMPT_HEADS)], axis=1)
-    lin[0] = dot(by_head(qs, PROMPT_HEADS), before, NN)
-    lin[1] = dot(by_head(cs, PROMPT_HEADS), before_wide, NT)
-    lin[2] = dot(by_head(pv[...], PROMPT_HEADS), after_wide, NT)
-    lin[3] = dot(by_head(pk[...], PROMPT_HEADS), after, NN)
-    mixings(qs, pk[...], PROMPT_HEADS, mix)
-    mixings(cs, pv[...], PROMPT_HEADS, gmix)
-    blocks(True, po, pdq, pdk, pdv, pq, pk, pv, pc, None)
-
-    weighted = reply_weighted(rc[...], weight[0], length[0])
-    first = NY * NX * (ROWS // PROMPT_HEADS)
-    qs = scale_rows(rq[...], first, REPLY_HEADS)
-    cs = scale_rows(weighted, first, REPLY_HEADS)
-    final = fin[...]
-    final_wide = jnp.concatenate(
-        [final[h * E:(h + 1) * E] for h in range(REPLY_HEADS)], axis=1)
-    lin[0] = dot(by_head(qs, REPLY_HEADS), final, NN)
-    lin[1] = dot(by_head(cs, REPLY_HEADS), final_wide, NT)
-    mixings(qs, rk[...], REPLY_HEADS, mix)
-    mixings(cs, rv[...], REPLY_HEADS, gmix)
-    blocks(False, ro, rdq, rdk, rdv, rq, rk, rv, weighted, length[0])
-
-
-def finish(pq, pk, pv, pc, rq, rk, rv, rc, bef, aft, fin, weight, length):
-    vmem = pl.BlockSpec(memory_space=pltpu.VMEM)
-    smem = pl.BlockSpec(memory_space=pltpu.SMEM)
+    ins = (aft_in, pv_in, pdk_in, pk_in, pdv_in, po_in, ro_in, pdq_in, rdq_in, rdk_in, rdv_in)
+    held = (aft, pv, kpart, pk, vpart, po, ro, pdq, rdq, rdk, rdv)
+    outs = (po_out, ro_out, pdq_out, rdq_out, rdk_out, rdv_out)
+    loads = [pltpu.make_async_copy(src, dst, in_sem.at[n])
+             for n, (src, dst) in enumerate(zip(ins, held))]
+    for load in loads:
+        load.start()
+    saves = []
+
+    def save(src, dst):
+        copy = pltpu.make_async_copy(src, dst, out_sem.at[len(saves)])
+        copy.start()
+        saves.append(copy)
+
+    loads[0].wait()
+    loads[1].wait()
+    wide = stack_wide(aft[...], PROMPT_HEADS)
+    grad = dot(by_head(pv[...], PROMPT_HEADS), wide, NT)
+    loads[2].wait()
+    pdk[...] = (kpart[...] + grad).astype(BF16)
+    save(pdk, pdk_out)
+    loads[3].wait()
+    grad = dot(by_head(pk[...], PROMPT_HEADS), aft[...], NN)
+    loads[4].wait()
+    pdv[...] = (vpart[...] + grad).astype(BF16)
+    save(pdv, pdv_out)
+    for n in range(6):
+        loads[5 + n].wait()
+        save(held[5 + n], outs[n])
+    for copy in saves:
+        copy.wait()
+
+
+def finish(*args):
+    whole = pl.BlockSpec(memory_space=pl.ANY)
+    narrow = pltpu.VMEM((ROWS, E), BF16)
+    wide = pltpu.VMEM((ROWS, E), F32)
     return pl.pallas_call(
         finish_kernel,
         out_shape=tuple([jax.ShapeDtypeStruct((ROWS, E), BF16)] * 8),
-        in_specs=[vmem] * 11 + [smem] * 2,
-        out_specs=tuple([vmem] * 8),
-        scratch_shapes=[
-            pltpu.VMEM((ROWS, ROWS), BF16),
-            pltpu.VMEM((ROWS, ROWS), BF16),
-            pltpu.VMEM((4, ROWS, E), F32),
-        ],
+        in_specs=[whole] * 11,
+        out_specs=tuple([whole] * 8),
+        scratch_shapes=[narrow] * 6 + [wide] * 2 + [
+            pltpu.VMEM((PROMPT_HEADS * E, E), BF16)] + [narrow] * 4 + [
+            pltpu.SemaphoreType.DMA((11,)), pltpu.SemaphoreType.DMA((8,))],
         name="finish",
-    )(pq, pk, pv, pc, rq, rk, rv, rc, bef, aft, fin, weight, length)
+    )(*args)
 
 
 def shards(
@@ -464,9 +523,8 @@
         for a in (prompt_query, prompt_key, prompt_value, prompt_cotangent,
                   reply_query, reply_key, reply_value, reply_cotangent)
     ]
-    bef, aft, fin = exchange(pq, pk, pv, pc, rq, rc, reply_weight, reply_length)
-    po, pdq, pdk, pdv, ro, rdq, rdk, rdv = finish(
-        pq, pk, pv, pc, rq, rk, rv, rc, bef, aft, fin, reply_weight, reply_length)
+    parts = exchange(pq, pk, pv, pc, rq, rk, rv, rc, reply_weight, reply_length)
+    po, ro, pdq, rdq, rdk, rdv, pdk, pdv = finish(*parts, pk, pv)
     return (
         po.reshape(prompt_shape), ro.reshape(reply_shape),
         pdq.reshape(prompt_shape), pdk.reshape(prompt_shape), pdv.reshape(prompt_shape),

time: 53.8 us -> 46.5 us (0.86)
  the two profiles are of different devices: /device:TPU:64 before, /device:TPU:1 now
where the time goes in v2:
time: 46.5 us; the launch traced here: 45.6 us
  Pallas kernels  43.7 us (94%)
  between operations  1.93 us (4%)
    pallas_call x1, Pallas kernels, exchange(): pl.pallas_call(exchange_kernel, out_shape=tuple([jax.ShapeDtypeStruct((RO...  40.3 us
    pallas_call x1, Pallas kernels, finish(): pl.pallas_call(finish_kernel, out_shape=tuple([jax.ShapeDtypeStruct((ROWS...  3.37 us

profile of v2, /device:TPU:1, one launch (start us, length us, event | category | flops | bytes accessed | tf_op | source)
XLA Modules:
  0.0 45.6 jit_solution(4881893568171241581)
XLA Ops:
  1.9 40.3 %exchange.1 = (bf16[1024,128]{1,0:T(8,128)(2,1)}, bf16[1024,128]{1,0:T(8,128)(2,1)}, bf16[1024,128]{1,0:T(8,128)(2,1)}, bf16[1024,128]{1,0:T(8,128)(2,1)}, bf16[...) custom-call(bf16[1024,128]{1,0:T(8,128)(2,1)} %bitcast.20, ...), custom_call_target="tpu_custom_call" | custom-call | tf_op jit(solution)/shard_map/exchange/pallas_call | solution.py:424
  42.2 3.4 %finish.1 = (bf16[1024,128]{1,0:T(8,128)(2,1)}, bf16[1024,128]{1,0:T(8,128)(2,1)}, bf16[1024,128]{1,0:T(8,128)(2,1)}, bf16[1024,128]{1,0:T(8,128)(2,1)}, bf16[10...) custom-call(bf16[1024,128]{1,0:T(8,128)(2,1)} %get-tuple-element.25.po_in, ...), custom_call_target="tpu_custom_call" | custom-call | tf_op jit(solution)/shard_map/finish/pallas_call | solution.py:502

commit v3 on v2

v3 whole, which is shorter than its diff:
```python
import jax
import jax.numpy as jnp
from jax import lax
from jax.experimental import pallas as pl
from jax.experimental.pallas import tpu as pltpu
from jax.sharding import PartitionSpec as P

MESH = pl.DeviceIdType.MESH
F32 = jnp.float32
BF16 = jnp.bfloat16
NY, NX, NZ, NC = 8, 4, 8, 2
E = 128
ROWS = 1024
PROMPT_HEADS = 4
REPLY_HEADS = 2
BLK = 256
SL = E // NY
FAR = [4, 3, 5, 2, 6, 1, 7, 0]
NEAR = [0, 1, 7, 2, 6, 3, 5, 4]

NN = (((1,), (0,)), ((), ()))
NT = (((1,), (1,)), ((), ()))
TN = (((0,), (0,)), ((), ()))


def dot(a, b, dims):
    return lax.dot_general(a, b, dims, preferred_element_type=F32)


def scale_rows(x, first, heads):
    s = lax.broadcasted_iota(jnp.int32, x.shape, 0)
    pos = (first + s // heads).astype(F32)
    return (x.astype(F32) * lax.rsqrt(float(E) * (pos + 1.0))).astype(BF16)


def by_head(x, heads):
    period = lax.broadcasted_iota(jnp.int32, (16, E), 0) & (heads - 1)
    tiles = x.reshape(ROWS // 16, 16, E)
    parts = []
    for h in range(heads):
        keep = jnp.where(period == h, 1.0, 0.0).astype(BF16)
        parts.append((tiles * keep[None]).reshape(ROWS, E))
    return jnp.concatenate(parts, axis=1)


def reply_weighted(c, weight, length):
    s = lax.broadcasted_iota(jnp.int32, c.shape, 0)
    live = (s // REPLY_HEADS) < length
    return (weight * jnp.where(live, c.astype(F32), 0.0)).astype(BF16)


def wait_bytes(view, sem):
    pltpu.make_async_copy(view, view, sem).wait()


def pair_masks(heads):
    a = lax.broadcasted_iota(jnp.int32, (BLK, BLK), 0)
    b = lax.broadcasted_iota(jnp.int32, (BLK, BLK), 1)
    same = ((a ^ b) & (heads - 1)) == 0
    off = jnp.where(same, 1.0, 0.0)
    diag = jnp.where(a >= b, off, 0.0)
    return off.astype(BF16), diag.astype(BF16)


def mixings(left, right, heads, dest):
    off, diag = pair_masks(heads)
    for i in range(ROWS // BLK):
        rows = pl.ds(i * BLK, BLK)
        for j in range(i + 1):
            cols = pl.ds(j * BLK, BLK)
            part = dot(left[i * BLK:(i + 1) * BLK], right[j * BLK:(j + 1) * BLK], NT)
            dest[rows, cols] = part.astype(BF16) * (diag if i == j else off)


def stack_wide(state, heads):
    return jnp.concatenate([state[h * E:(h + 1) * E] for h in range(heads)], axis=1)


def exchange_kernel(
    pq_in, pk_in, pv_in, pc_in, rq_in, rk_in, rv_in, rc_in, weight, length,
    po_out, ro_out, pdq_out, rdq_out, rdk_out, rdv_out, pdk_out, pdv_out, aft_out,
    pq, pk, pv, pc, rq, rk, rv, rc,
    po, ro, pdq, rdq, rdk, rdv, pdk, pdv, aft, bef,
    pqs, pcs, rqs, rcs, rw, mix, gmix, part,
    raw, loc, xr, yt, yr, ys, yb, xs, st, tot, fin, wl, wy, wq, wt, wf,
    in_sem, out_sem,
    x_send, x_recv, y_send, y_recv, b_send, b_recv, s_send, s_recv,
    f_send, f_recv, w_send, w_recv, v_send, v_recv, u_send, u_recv,
):
    y = lax.axis_index("ctx")
    x = lax.axis_index("head")
    r = lax.axis_index("resp")
    z = r // 2
    c = r % 2
    fx = 2 * c + x // 2
    wc = x // 2
    wx = 2 * (x % 2)
    same_column = fx == x
    loops_back = same_column & (z == y)
    gathers = c == wc

    barrier = pltpu.get_barrier_semaphore()

    loads = [
        pltpu.make_async_copy(src, dst, in_sem.at[n])
        for n, (src, dst) in enumerate((
            (pk_in, pk), (pv_in, pv), (rq_in, rq), (rc_in, rc),
            (pq_in, pq), (pc_in, pc), (rk_in, rk), (rv_in, rv)))
    ]
    for load in loads:
        load.start()

    saves = []

    def save(src, dst):
        copy = pltpu.make_async_copy(src, dst, out_sem.at[len(saves)])
        copy.start()
        saves.append(copy)

    def send(src, dst, send_sem, recv_sem, device):
        pltpu.make_async_remote_copy(
            src_ref=src, dst_ref=dst, send_sem=send_sem, recv_sem=recv_sem,
            device_id=device, device_id_type=MESH).start()

    def signal(device):
        pl.semaphore_signal(barrier, inc=1, device_id=device, device_id_type=MESH)

    @pl.loop(1, NX)
    def _(d):
        signal((y, (x + d) % NX, r))

    @pl.loop(1, NY)
    def _(d):
        signal(((y + d) % NY, x, r))

    @pl.loop(1, NZ * NC)
    def _(d):
        signal((y, x, (r + d) % (NZ * NC)))

    block = y * NX + x
    prompt_first = block * (ROWS // PROMPT_HEADS)
    reply_first = NY * NX * (ROWS // PROMPT_HEADS)

    def states(k, left, right):
        wide = dot(left, by_head(right, PROMPT_HEADS), TN)
        for h in range(PROMPT_HEADS):
            raw[h] = wide[:, h * E:(h + 1) * E].reshape(NY, SL, E)
        for p in range(NY):
            row = (y + FAR[p]) % NY
            for h in range(PROMPT_HEADS):
                loc[k, h, p] = raw[h, row]

    def x_start(k):
        for piece in range(NY // 2):
            span = pl.ds(2 * piece, 2)

            @pl.loop(1, NX)
            def _(d):
                to = (x + d) % NX
                send(loc.at[k, to, span], xr.at[k, x, span],
                     x_send.at[k], x_recv.at[k, piece], (y, to, r))
        xr[k, x] = loc[k, x]

    def y_piece(k, piece):
        wait_bytes(xr.at[k, 0, pl.ds(0, 2 * (NX - 1))], x_recv.at[k, piece])
        for p in (2 * piece, 2 * piece + 1):
            yt[k, p] = (xr[k, 0, p] + xr[k, 1, p]) + (xr[k, 2, p] + xr[k, 3, p])
            if FAR[p]:
                send(yt.at[k, p], yr.at[k, y], y_send.at[k], y_recv.at[k],
                     ((y + FAR[p]) % NY, x, r))
            else:
                yr[k, y] = yt[k, p]

    def b_start(k):
        for rel in FAR[:-1]:
            to = (y + rel) % NY
            back = (NY - rel) % NY
            send(ys.at[k, to], yb.at[k, NEAR.index(back)],
                 b_send.at[k], b_recv.at[k, min(back, NY - back) - 1], (to, x, r))
        yb[k, 0] = ys[k, y]

    def s_piece(k, piece):
        first, count = ((0, 3), (3, 2), (5, 2), (7, 1))[piece]
        wait_bytes(yb.at[k, pl.ds(0, 1 if piece == 3 else 2)], b_recv.at[k, piece])
        for q in range(first, first + count):
            p = FAR.index(NEAR[q])
            running = yb[k, q]
            order = range(NX) if k == 0 else range(NX - 1, -1, -1)
            for n in order:
                xs[k, n, q] = running
                running = running + xr[k, n, p]
        span = pl.ds(first, count)

        @pl.loop(1, NX)
        def _(d):
            to = (x + d) % NX
            send(xs.at[k, to, span], st.at[k, x, span],
                 s_send.at[k], s_recv.at[k], (y, to, r))
        for q in range(first, first + count):
            st[k, x, q] = xs[k, x, q]

    def collect(k, dest):
        wait_bytes(st.at[k, pl.ds(0, NX - 1)], s_recv.at[k])
        for q in range(NY):
            row = (y + NEAR[q]) % NY
            for h in range(PROMPT_HEADS):
                dest[h, row] = st[k, h, q].astype(BF16)

    loads[0].wait()
    loads[1].wait()
    states(0, pk[...], pv[...])

    loads[2].wait()
    loads[3].wait()
    rw[...] = reply_weighted(rc[...], weight[0], length[0])
    rqs[...] = scale_rows(rq[...], reply_first, REPLY_HEADS)
    wide = dot(rqs[...], by_head(rw[...], REPLY_HEADS), TN)
    for i in range(REPLY_HEADS):
        moment = wide[:, i * E:(i + 1) * E].reshape(NY, SL, E)
        for n in range(NY):
            wl[n, i] = moment[n]

    pl.semaphore_wait(barrier, NX - 1 + NY - 1 + NZ * NC - 1)
    x_start(0)
    for rel in FAR[:-1]:
        to = (y + rel) % NY
        send(wl.at[to], wy.at[y], w_send, w_recv, (to, x, r))
    wy[y] = wl[y]

    loads[4].wait()
    loads[5].wait()
    pqs[...] = scale_rows(pq[...], prompt_first, PROMPT_HEADS)
    states(1, pqs[...], pc[...])
    x_start(1)

    blocks = [(slice(i * BLK, (i + 1) * BLK), slice(0, (i + 1) * BLK), slice(i * BLK, ROWS))
              for i in range(ROWS // BLK)]

    mixings(pqs, pk, PROMPT_HEADS, mix)

    for piece in range(NY // 2):
        y_piece(0, piece)

    wait_bytes(wy.at[pl.ds(0, NY - 1)], w_recv)

    @pl.loop(0, NZ)
    def _(n):
        to = 2 * n + wc

        @pl.when(to != r)
        def _():
            send(wy.at[n], wq.at[r], v_send, v_recv, (y, x, to))

    @pl.when(gathers)
    def _():
        wq[r] = wy[z]

    for piece in range(NY // 2):
        y_piece(1, piece)

    wait_bytes(yr.at[0, pl.ds(0, NY - 1)], y_recv.at[0])
    running = jnp.zeros((SL, E), F32)
    for n in range(NY):
        ys[0, n] = running
        running = running + yr[0, n]
    tot[...] = running
    b_start(0)

    @pl.loop(0, NZ * NC)
    def _(n):
        to = (2 * z + NZ + n) % (NZ * NC)

        @pl.when(jnp.logical_not(loops_back & (to == r)))
        def _():
            send(tot, fin.at[(x % 2) * NY + y], f_send, f_recv, (z, fx, to))

    @pl.when(loops_back)
    def _():
        fin[(x % 2) * NY + y] = tot[...]

    pcs[...] = scale_rows(pc[...], prompt_first, PROMPT_HEADS)
    mixings(pcs, pv, PROMPT_HEADS, gmix)

    s_piece(0, 0)
    s_piece(0, 1)

    @pl.when(gathers)
    def _():
        wait_bytes(wq.at[pl.ds(0, NZ * NC - 1)], v_recv)
        total = wq[0]
        for n in range(1, NZ * NC):
            total = total + wq[n]
        wt[...] = total

        @pl.loop(0, REPLY_HEADS)
        def _(i):
            @pl.when(wx + i != x)
            def _():
                send(wt.at[i], wf, u_send, u_recv, (y, wx + i, r))

        @pl.when(same_column)
        def _():
            wf[...] = wt[x % 2]

    s_piece(0, 2)
    s_piece(0, 3)

    wait_bytes(yr.at[1, pl.ds(0, NY - 1)], y_recv.at[1])

    @pl.when(jnp.logical_not(same_column))
    def _():
        wait_bytes(wf, u_recv)

    running = wf[...]
    for n in reversed(range(NY)):
        ys[1, n] = running
        running = running + yr[1, n]
    b_start(1)

    for rows, upto, onward in blocks:
        pdk[rows] = dot(gmix[onward, rows], pq[onward], TN)
        pdv[rows] = dot(mix[onward, rows], pc[onward], TN)
    save(pdk, pdk_out)
    save(pdv, pdv_out)

    s_piece(1, 0)
    s_piece(1, 1)
    s_piece(1, 2)
    s_piece(1, 3)

    for rows, upto, onward in blocks:
        part[0, rows] = dot(mix[rows, upto], pv[upto], NN)
        part[1, rows] = dot(gmix[rows, upto], pk[upto], NN)
    loads[6].wait()
    loads[7].wait()
    mixings(rqs, rk, REPLY_HEADS, mix)
    rcs[...] = scale_rows(rw[...], reply_first, REPLY_HEADS)
    mixings(rcs, rv, REPLY_HEADS, gmix)
    for rows, upto, onward in blocks:
        rdv[rows] = dot(mix[onward, rows], rw[onward], TN).astype(BF16)
    save(rdv, rdv_out)
    for rows, upto, onward in blocks:
        rdk[rows] = dot(gmix[onward, rows], rq[onward], TN).astype(BF16)
    save(rdk, rdk_out)
    for rows, upto, onward in blocks:
        part[2, rows] = dot(mix[rows, upto], rv[upto], NN)
        part[3, rows] = dot(gmix[rows, upto], rk[upto], NN)

    collect(0, bef)
    before = bef[...].reshape(PROMPT_HEADS * E, E)
    po[...] = (part[0] + dot(by_head(pqs[...], PROMPT_HEADS), before, NN)).astype(BF16)
    save(po, po_out)
    wide = stack_wide(before, PROMPT_HEADS)
    pdq[...] = (part[1] + dot(by_head(pcs[...], PROMPT_HEADS), wide, NT)).astype(BF16)
    save(pdq, pdq_out)

    collect(1, aft)
    save(aft, aft_out)

    @pl.when(loops_back)
    def _():
        wait_bytes(fin.at[pl.ds(0, 15)], f_recv)

    @pl.when(jnp.logical_not(loops_back))
    def _():
        wait_bytes(fin, f_recv)

    final = fin[...].reshape(REPLY_HEADS * E, E).astype(BF16)
    out = part[2] + dot(by_head(rqs[...], REPLY_HEADS), final, NN)
    s = lax.broadcasted_iota(jnp.int32, (ROWS, E), 0)
    ro[...] = jnp.where((s // REPLY_HEADS) < length[0], out, 0.0).astype(BF16)
    save(ro, ro_out)
    wide = stack_wide(final, REPLY_HEADS)
    rdq[...] = (part[3] + dot(by_head(rcs[...], REPLY_HEADS), wide, NT)).astype(BF16)
    save(rdq, rdq_out)

    for k in range(2):
        wait_bytes(loc.at[k, pl.ds(0, NX - 1)], x_send.at[k])
        wait_bytes(yt.at[k, pl.ds(0, NY - 1)], y_send.at[k])
        wait_bytes(ys.at[k, pl.ds(0, NY - 1)], b_send.at[k])
        wait_bytes(xs.at[k, pl.ds(0, NX - 1)], s_send.at[k])
    wait_bytes(wl.at[pl.ds(0, NY - 1)], w_send)

    @pl.when(loops_back)
    def _():
        wait_bytes(fin.at[pl.ds(0, 15)], f_send)

    @pl.when(jnp.logical_not(loops_back))
    def _():
        wait_bytes(fin, f_send)

    @pl.when(gathers)
    def _():
        wait_bytes(wy.at[pl.ds(0, NZ - 1)], v_send)

        @pl.when(same_column)
        def _():
            wait_bytes(wt.at[0], u_send)

        @pl.when(jnp.logical_not(same_column))
        def _():
            wait_bytes(wt, u_send)

    @pl.when(jnp.logical_not(gathers))
    def _():
        wait_bytes(wy, v_send)

    for copy in saves:
        copy.wait()


def exchange(*args):
    whole = pl.BlockSpec(memory_space=pl.ANY)
    smem = pl.BlockSpec(memory_space=pltpu.SMEM)
    dma = pltpu.SemaphoreType.DMA
    heads = pltpu.VMEM((2, NX, NY, SL, E), F32)
    narrow = pltpu.VMEM((ROWS, E), BF16)
    wide = pltpu.VMEM((ROWS, E), F32)
    slices = pltpu.VMEM((2, NY, SL, E), F32)
    return pl.pallas_call(
        exchange_kernel,
        out_shape=tuple(
            [jax.ShapeDtypeStruct((ROWS, E), BF16)] * 6
            + [jax.ShapeDtypeStruct((ROWS, E), F32)] * 2
            + [jax.ShapeDtypeStruct((PROMPT_HEADS, NY, SL, E), BF16)]),
        in_specs=[whole] * 8 + [smem] * 2,
        out_specs=tuple([whole] * 9),
        scratch_shapes=[narrow] * 14 + [wide] * 2 + [
            pltpu.VMEM((PROMPT_HEADS, NY, SL, E), BF16),
            pltpu.VMEM((PROMPT_HEADS, NY, SL, E), BF16),
        ] + [narrow] * 5 + [
            pltpu.VMEM((ROWS, ROWS), BF16),
            pltpu.VMEM((ROWS, ROWS), BF16),
            pltpu.VMEM((4, ROWS, E), F32),
            pltpu.VMEM((NX, NY, SL, E), F32),
            heads, heads,
            slices, slices, slices, slices,
            heads, heads,
            pltpu.VMEM((SL, E), F32),
            pltpu.VMEM((16, SL, E), F32),
            pltpu.VMEM((NY, 2, SL, E), F32),
            pltpu.VMEM((NY, 2, SL, E), F32),
            pltpu.VMEM((16, 2, SL, E), F32),
            pltpu.VMEM((2, SL, E), F32),
            pltpu.VMEM((SL, E), F32),
            dma((8,)), dma((9,)),
            dma((2,)), dma((2, 4)), dma((2,)), dma((2,)),
            dma((2,)), dma((2, 4)), dma((2,)), dma((2,)),
            dma, dma, dma, dma, dma, dma, dma, dma,
        ],
        compiler_params=pltpu.CompilerParams(
            collective_id=0, has_side_effects=True),
        name="exchange",
    )(*args)


def finish_kernel(
    po_in, ro_in, pdq_in, rdq_in, rdk_in, rdv_in, pdk_in, pdv_in, aft_in, pk_in, pv_in,
    po_out, ro_out, pdq_out, rdq_out, rdk_out, rdv_out, pdk_out, pdv_out,
    po, ro, pdq, rdq, rdk, rdv, kpart, vpart, aft, pk, pv, pdk, pdv, in_sem, out_sem,
):
    ins = (aft_in, pv_in, pdk_in, pk_in, pdv_in, po_in, ro_in, pdq_in, rdq_in, rdk_in, rdv_in)
    held = (aft, pv, kpart, pk, vpart, po, ro, pdq, rdq, rdk, rdv)
    outs = (po_out, ro_out, pdq_out, rdq_out, rdk_out, rdv_out)
    loads = [pltpu.make_async_copy(src, dst, in_sem.at[n])
             for n, (src, dst) in enumerate(zip(ins, held))]
    for load in loads:
        load.start()
    saves = []

    def save(src, dst):
        copy = pltpu.make_async_copy(src, dst, out_sem.at[len(saves)])
        copy.start()
        saves.append(copy)

    loads[0].wait()
    loads[1].wait()
    wide = stack_wide(aft[...], PROMPT_HEADS)
    grad = dot(by_head(pv[...], PROMPT_HEADS), wide, NT)
    loads[2].wait()
    pdk[...] = (kpart[...] + grad).astype(BF16)
    save(pdk, pdk_out)
    loads[3].wait()
    grad = dot(by_head(pk[...], PROMPT_HEADS), aft[...], NN)
    loads[4].wait()
    pdv[...] = (vpart[...] + grad).astype(BF16)
    save(pdv, pdv_out)
    for n in range(6):
        loads[5 + n].wait()
        save(held[5 + n], outs[n])
    for copy in saves:
        copy.wait()


def finish(*args):
    whole = pl.BlockSpec(memory_space=pl.ANY)
    narrow = pltpu.VMEM((ROWS, E), BF16)
    wide = pltpu.VMEM((ROWS, E), F32)
    return pl.pallas_call(
        finish_kernel,
        out_shape=tuple([jax.ShapeDtypeStruct((ROWS, E), BF16)] * 8),
        in_specs=[whole] * 11,
        out_specs=tuple([whole] * 8),
        scratch_shapes=[narrow] * 6 + [wide] * 2 + [
            pltpu.VMEM((PROMPT_HEADS * E, E), BF16)] + [narrow] * 4 + [
            pltpu.SemaphoreType.DMA((11,)), pltpu.SemaphoreType.DMA((8,))],
        name="finish",
    )(*args)


def shards(
    prompt_query, prompt_key, prompt_value, prompt_cotangent,
    reply_query, reply_key, reply_value, reply_cotangent,
    reply_weight, reply_length,
):
    prompt_shape = prompt_query.shape
    reply_shape = reply_query.shape
    pq, pk, pv, pc, rq, rk, rv, rc = [
        a.reshape(ROWS, E)
        for a in (prompt_query, prompt_key, prompt_value, prompt_cotangent,
                  reply_query, reply_key, reply_value, reply_cotangent)
    ]
    parts = exchange(pq, pk, pv, pc, rq, rk, rv, rc, reply_weight, reply_length)
    after = parts[-1].reshape(PROMPT_HEADS * E, E)
    po, ro, pdq, rdq, rdk, rdv, pdk, pdv = finish(*parts[:-1], after, pk, pv)
    return (
        po.reshape(prompt_shape), ro.reshape(reply_shape),
        pdq.reshape(prompt_shape), pdk.reshape(prompt_shape), pdv.reshape(prompt_shape),
        rdq.reshape(reply_shape), rdk.reshape(reply_shape), rdv.reshape(reply_shape),
    )


def solution(mesh):
    prompt = P(("ctx", "head"), "resp", None)
    reply = P("resp", None, ("ctx", "head"), None)
    placed = (prompt,) * 4 + (reply,) * 4 + (P("resp"), P("resp"))
    return jax.shard_map(
        shards,
        mesh=mesh,
        in_specs=placed,
        out_specs=(prompt, reply, prompt, prompt, prompt, reply, reply, reply),
        check_vma=False,
    )
```

time: 46.5 us -> 51.1 us (1.099)
  the two profiles are of different devices: /device:TPU:1 before, /device:TPU:192 now
where the time goes in v3:
time: 51.1 us; the launch traced here: 50.9 us
  Pallas kernels  49 us (96%)
  between operations  1.93 us (4%)
    pallas_call x1, Pallas kernels, exchange(): pl.pallas_call(exchange_kernel, out_shape=tuple([jax.ShapeDtypeStruct((RO...  45.6 us
    pallas_call x1, Pallas kernels, finish(): pl.pallas_call(finish_kernel, out_shape=tuple([jax.ShapeDtypeStruct((ROWS...  3.37 us

profile of v3, /device:TPU:192, one launch (start us, length us, event | category | flops | bytes accessed | tf_op | source)
XLA Modules:
  0.0 50.9 jit_solution(8568096193247805369)
XLA Ops:
  1.9 45.6 %exchange.1 = (bf16[1024,128]{1,0:T(8,128)(2,1)}, bf16[1024,128]{1,0:T(8,128)(2,1)}, bf16[1024,128]{1,0:T(8,128)(2,1)}, bf16[1024,128]{1,0:T(8,128)(2,1)}, bf16[...) custom-call(bf16[1024,128]{1,0:T(8,128)(2,1)} %bitcast.21, ...), custom_call_target="tpu_custom_call" | custom-call | tf_op jit(solution)/shard_map/exchange/pallas_call | solution.py:420
  47.6 3.4 %finish.1 = (bf16[1024,128]{1,0:T(8,128)(2,1)}, bf16[1024,128]{1,0:T(8,128)(2,1)}, bf16[1024,128]{1,0:T(8,128)(2,1)}, bf16[1024,128]{1,0:T(8,128)(2,1)}, bf16[10...) custom-call(bf16[1024,128]{1,0:T(8,128)(2,1)} %get-tuple-element.25.po_in, ...), custom_call_target="tpu_custom_call" | custom-call | tf_op jit(solution)/shard_map/finish/pallas_call | solution.py:499

commit v4 on v3

--- a/solution.py
+++ b/solution.py
@@ -82,10 +82,10 @@
     pq, pk, pv, pc, rq, rk, rv, rc,
     po, ro, pdq, rdq, rdk, rdv, pdk, pdv, aft, bef,
     pqs, pcs, rqs, rcs, rw, mix, gmix, part,
-    raw, loc, xr, yt, yr, ys, yb, xs, st, tot, fin, wl, wy, wq, wt, wf,
+    raw, loc, xr, yt, yr, ys, yb, xs, st, zf, fin, wl, wp, ws, wy, wq, wt, wf,
     in_sem, out_sem,
     x_send, x_recv, y_send, y_recv, b_send, b_recv, s_send, s_recv,
-    f_send, f_recv, w_send, w_recv, v_send, v_recv, u_send, u_recv,
+    z_send, z_recv, f_send, f_recv, w_send, w_recv, v_send, v_recv, u_send, u_recv, c_send, c_recv,
 ):
     y = lax.axis_index("ctx")
     x = lax.axis_index("head")
@@ -93,11 +93,9 @@
     z = r // 2
     c = r % 2
     fx = 2 * c + x // 2
-    wc = x // 2
-    wx = 2 * (x % 2)
     same_column = fx == x
-    loops_back = same_column & (z == y)
-    gathers = c == wc
+    owner = (y, 2 * (x % 2) + c, 2 * z + x // 2)
+    summer = (y, fx, 2 * z + x % 2)
 
     barrier = pltpu.get_barrier_semaphore()
 
@@ -136,6 +134,11 @@
     @pl.loop(1, NZ * NC)
     def _(d):
         signal((y, x, (r + d) % (NZ * NC)))
+
+    @pl.when(jnp.logical_not(same_column))
+    def _():
+        signal(owner)
+        signal(summer)
 
     block = y * NX + x
     prompt_first = block * (ROWS // PROMPT_HEADS)
@@ -216,16 +219,20 @@
     rqs[...] = scale_rows(rq[...], reply_first, REPLY_HEADS)
     wide = dot(rqs[...], by_head(rw[...], REPLY_HEADS), TN)
     for i in range(REPLY_HEADS):
-        moment = wide[:, i * E:(i + 1) * E].reshape(NY, SL, E)
-        for n in range(NY):
-            wl[n, i] = moment[n]
-
-    pl.semaphore_wait(barrier, NX - 1 + NY - 1 + NZ * NC - 1)
+        wl[i] = wide[:, i * E:(i + 1) * E].reshape(NY, SL, E)
+
+    near = NX - 1 + NY - 1 + NZ * NC - 1
+
+    @pl.when(same_column)
+    def _():
+        pl.semaphore_wait(barrier, near)
+
+    @pl.when(jnp.logical_not(same_column))
+    def _():
+        pl.semaphore_wait(barrier, near + 2)
+
+    send(wl.at[1 - c], wp, c_send, c_recv, (y, x, 2 * z + 1 - c))
     x_start(0)
-    for rel in FAR[:-1]:
-        to = (y + rel) % NY
-        send(wl.at[to], wy.at[y], w_send, w_recv, (to, x, r))
-    wy[y] = wl[y]
 
     loads[4].wait()
     loads[5].wait()
@@ -233,6 +240,13 @@
     states(1, pqs[...], pc[...])
     x_start(1)
 
+    wait_bytes(wp, c_recv)
+    ws[...] = wl[c] + wp[...]
+    for rel in FAR[:-1]:
+        to = (y + rel) % NY
+        send(ws.at[to], wy.at[y], w_send, w_recv, (to, x, r))
+    wy[y] = ws[y]
+
     blocks = [(slice(i * BLK, (i + 1) * BLK), slice(0, (i + 1) * BLK), slice(i * BLK, ROWS))
               for i in range(ROWS // BLK)]
 
@@ -242,18 +256,10 @@
         y_piece(0, piece)
 
     wait_bytes(wy.at[pl.ds(0, NY - 1)], w_recv)
-
-    @pl.loop(0, NZ)
-    def _(n):
-        to = 2 * n + wc
-
-        @pl.when(to != r)
-        def _():
-            send(wy.at[n], wq.at[r], v_send, v_recv, (y, x, to))
-
-    @pl.when(gathers)
-    def _():
-        wq[r] = wy[z]
+    for rel in FAR[:-1]:
+        to = (z + rel) % NZ
+        send(wy.at[to], wq.at[z], v_send, v_recv, (y, x, 2 * to + c))
+    wq[z] = wy[z]
 
     for piece in range(NY // 2):
         y_piece(1, piece)
@@ -263,47 +269,43 @@
     for n in range(NY):
         ys[0, n] = running
         running = running + yr[0, n]
-    tot[...] = running
+    zf[z] = running
     b_start(0)
 
-    @pl.loop(0, NZ * NC)
-    def _(n):
-        to = (2 * z + NZ + n) % (NZ * NC)
-
-        @pl.when(jnp.logical_not(loops_back & (to == r)))
-        def _():
-            send(tot, fin.at[(x % 2) * NY + y], f_send, f_recv, (z, fx, to))
-
-    @pl.when(loops_back)
-    def _():
-        fin[(x % 2) * NY + y] = tot[...]
+    @pl.loop(1, NZ)
+    def _(d):
+        send(zf.at[z], zf.at[z], z_send, z_recv, (y, x, 2 * ((z + d) % NZ) + c))
 
     pcs[...] = scale_rows(pc[...], prompt_first, PROMPT_HEADS)
     mixings(pcs, pv, PROMPT_HEADS, gmix)
+    for rows, upto, onward in blocks:
+        part[0, rows] = dot(mix[rows, upto], pv[upto], NN)
+        part[1, rows] = dot(gmix[rows, upto], pk[upto], NN)
 
     s_piece(0, 0)
+    wait_bytes(wq.at[pl.ds(0, NZ - 1)], v_recv)
+    total = wq[0]
+    for n in range(1, NZ):
+        total = total + wq[n]
+    wt[...] = total
+
+    @pl.when(jnp.logical_not(same_column))
+    def _():
+        send(wt, wf, u_send, u_recv, owner)
+
+    @pl.when(same_column)
+    def _():
+        wf[...] = wt[...]
+
     s_piece(0, 1)
-
-    @pl.when(gathers)
-    def _():
-        wait_bytes(wq.at[pl.ds(0, NZ * NC - 1)], v_recv)
-        total = wq[0]
-        for n in range(1, NZ * NC):
-            total = total + wq[n]
-        wt[...] = total
-
-        @pl.loop(0, REPLY_HEADS)
-        def _(i):
-            @pl.when(wx + i != x)
-            def _():
-                send(wt.at[i], wf, u_send, u_recv, (y, wx + i, r))
-
-        @pl.when(same_column)
-        def _():
-            wf[...] = wt[x % 2]
-
     s_piece(0, 2)
     s_piece(0, 3)
+
+    for rows, upto, onward in blocks:
+        pdk[rows] = dot(gmix[onward, rows], pq[onward], TN)
+        pdv[rows] = dot(mix[onward, rows], pc[onward], TN)
+    save(pdk, pdk_out)
+    save(pdv, pdv_out)
 
     wait_bytes(yr.at[1, pl.ds(0, NY - 1)], y_recv.at[1])
 
@@ -317,23 +319,31 @@
         running = running + yr[1, n]
     b_start(1)
 
-    for rows, upto, onward in blocks:
-        pdk[rows] = dot(gmix[onward, rows], pq[onward], TN)
-        pdv[rows] = dot(mix[onward, rows], pc[onward], TN)
-    save(pdk, pdk_out)
-    save(pdv, pdv_out)
+    wait_bytes(zf.at[pl.ds(0, NZ - 1)], z_recv)
+    for rel in FAR:
+        row = (y + rel) % NY
+        for core in range(NC):
+            def go():
+                send(zf.at[row], fin.at[(x % 2) * NY + y], f_send, f_recv,
+                     (row, fx, 2 * z + core))
+            if rel:
+                go()
+            else:
+                pl.when(jnp.logical_not(same_column & (c == core)))(go)
+
+    @pl.when(same_column)
+    def _():
+        fin[(x % 2) * NY + y] = zf[y]
+
+    loads[6].wait()
+    loads[7].wait()
+    mixings(rqs, rk, REPLY_HEADS, mix)
 
     s_piece(1, 0)
     s_piece(1, 1)
     s_piece(1, 2)
     s_piece(1, 3)
 
-    for rows, upto, onward in blocks:
-        part[0, rows] = dot(mix[rows, upto], pv[upto], NN)
-        part[1, rows] = dot(gmix[rows, upto], pk[upto], NN)
-    loads[6].wait()
-    loads[7].wait()
-    mixings(rqs, rk, REPLY_HEADS, mix)
     rcs[...] = scale_rows(rw[...], reply_first, REPLY_HEADS)
     mixings(rcs, rv, REPLY_HEADS, gmix)
     for rows, upto, onward in blocks:
@@ -357,11 +367,11 @@
     collect(1, aft)
     save(aft, aft_out)
 
-    @pl.when(loops_back)
+    @pl.when(same_column)
     def _():
         wait_bytes(fin.at[pl.ds(0, 15)], f_recv)
 
-    @pl.when(jnp.logical_not(loops_back))
+    @pl.when(jnp.logical_not(same_column))
     def _():
         wait_bytes(fin, f_recv)
 
@@ -379,31 +389,19 @@
         wait_bytes(yt.at[k, pl.ds(0, NY - 1)], y_send.at[k])
         wait_bytes(ys.at[k, pl.ds(0, NY - 1)], b_send.at[k])
         wait_bytes(xs.at[k, pl.ds(0, NX - 1)], s_send.at[k])
-    wait_bytes(wl.at[pl.ds(0, NY - 1)], w_send)
-
-    @pl.when(loops_back)
+    wait_bytes(wp, c_send)
+    wait_bytes(wy.at[pl.ds(0, NY - 1)], w_send)
+    wait_bytes(wq.at[pl.ds(0, NZ - 1)], v_send)
+    wait_bytes(zf.at[pl.ds(0, NZ - 1)], z_send)
+
+    @pl.when(same_column)
     def _():
         wait_bytes(fin.at[pl.ds(0, 15)], f_send)
 
-    @pl.when(jnp.logical_not(loops_back))
+    @pl.when(jnp.logical_not(same_column))
     def _():
         wait_bytes(fin, f_send)
-
-    @pl.when(gathers)
-    def _():
-        wait_bytes(wy.at[pl.ds(0, NZ - 1)], v_send)
-
-        @pl.when(same_column)
-        def _():
-            wait_bytes(wt.at[0], u_send)
-
-        @pl.when(jnp.logical_not(same_column))
-        def _():
-            wait_bytes(wt, u_send)
-
-    @pl.when(jnp.logical_not(gathers))
-    def _():
-        wait_bytes(wy, v_send)
+        wait_bytes(wt, u_send)
 
     for copy in saves:
         copy.wait()
@@ -436,17 +434,19 @@
             heads, heads,
             slices, slices, slices, slices,
             heads, heads,
+            pltpu.VMEM((NZ, SL, E), F32),
+            pltpu.VMEM((16, SL, E), F32),
+            slices,
+            pltpu.VMEM((NY, SL, E), F32),
+            pltpu.VMEM((NY, SL, E), F32),
+            pltpu.VMEM((NY, SL, E), F32),
+            pltpu.VMEM((NZ, SL, E), F32),
             pltpu.VMEM((SL, E), F32),
-            pltpu.VMEM((16, SL, E), F32),
-            pltpu.VMEM((NY, 2, SL, E), F32),
-            pltpu.VMEM((NY, 2, SL, E), F32),
-            pltpu.VMEM((16, 2, SL, E), F32),
-            pltpu.VMEM((2, SL, E), F32),
             pltpu.VMEM((SL, E), F32),
             dma((8,)), dma((9,)),
             dma((2,)), dma((2, 4)), dma((2,)), dma((2,)),
             dma((2,)), dma((2, 4)), dma((2,)), dma((2,)),
-            dma, dma, dma, dma, dma, dma, dma, dma,
+            dma, dma, dma, dma, dma, dma, dma, dma, dma, dma, dma, dma,
         ],
         compiler_params=pltpu.CompilerParams(
             collective_id=0, has_side_effects=True),

time: 51.1 us -> 46.7 us (0.914)
  the two profiles are of different devices: /device:TPU:192 before, /device:TPU:1 now
where the time goes in v4:
time: 46.7 us; the launch traced here: 46.6 us
  Pallas kernels  44.6 us (96%)
  between operations  1.93 us (4%)
    pallas_call x1, Pallas kernels, exchange(): pl.pallas_call(exchange_kernel, out_shape=tuple([jax.ShapeDtypeStruct((RO...  41.2 us
    pallas_call x1, Pallas kernels, finish(): pl.pallas_call(finish_kernel, out_shape=tuple([jax.ShapeDtypeStruct((ROWS...  3.37 us

profile of v4, /device:TPU:1, one launch (start us, length us, event | category | flops | bytes accessed | tf_op | source)
XLA Modules:
  0.0 46.6 jit_solution(9934319772342794592)
XLA Ops:
  1.9 41.2 %exchange.1 = (bf16[1024,128]{1,0:T(8,128)(2,1)}, bf16[1024,128]{1,0:T(8,128)(2,1)}, bf16[1024,128]{1,0:T(8,128)(2,1)}, bf16[1024,128]{1,0:T(8,128)(2,1)}, bf16[...) custom-call(bf16[1024,128]{1,0:T(8,128)(2,1)} %bitcast.21, ...), custom_call_target="tpu_custom_call" | custom-call | tf_op jit(solution)/shard_map/exchange/pallas_call | solution.py:418
  43.2 3.4 %finish.1 = (bf16[1024,128]{1,0:T(8,128)(2,1)}, bf16[1024,128]{1,0:T(8,128)(2,1)}, bf16[1024,128]{1,0:T(8,128)(2,1)}, bf16[1024,128]{1,0:T(8,128)(2,1)}, bf16[10...) custom-call(bf16[1024,128]{1,0:T(8,128)(2,1)} %get-tuple-element.25.po_in, ...), custom_call_target="tpu_custom_call" | custom-call | tf_op jit(solution)/shard_map/finish/pallas_call | solution.py:499

commit v5 on v4

--- a/solution.py
+++ b/solution.py
@@ -252,7 +252,7 @@
 
     mixings(pqs, pk, PROMPT_HEADS, mix)
 
-    for piece in range(NY // 2):
+    for piece in range(3):
         y_piece(0, piece)
 
     wait_bytes(wy.at[pl.ds(0, NY - 1)], w_recv)
@@ -261,6 +261,7 @@
         send(wy.at[to], wq.at[z], v_send, v_recv, (y, x, 2 * to + c))
     wq[z] = wy[z]
 
+    y_piece(0, 3)
     for piece in range(NY // 2):
         y_piece(1, piece)
 
@@ -278,11 +279,7 @@
 
     pcs[...] = scale_rows(pc[...], prompt_first, PROMPT_HEADS)
     mixings(pcs, pv, PROMPT_HEADS, gmix)
-    for rows, upto, onward in blocks:
-        part[0, rows] = dot(mix[rows, upto], pv[upto], NN)
-        part[1, rows] = dot(gmix[rows, upto], pk[upto], NN)
-
-    s_piece(0, 0)
+
     wait_bytes(wq.at[pl.ds(0, NZ - 1)], v_recv)
     total = wq[0]
     for n in range(1, NZ):
@@ -297,15 +294,14 @@
     def _():
         wf[...] = wt[...]
 
+    for rows, upto, onward in blocks:
+        part[0, rows] = dot(mix[rows, upto], pv[upto], NN)
+        part[1, rows] = dot(gmix[rows, upto], pk[upto], NN)
+
+    s_piece(0, 0)
     s_piece(0, 1)
     s_piece(0, 2)
     s_piece(0, 3)
-
-    for rows, upto, onward in blocks:
-        pdk[rows] = dot(gmix[onward, rows], pq[onward], TN)
-        pdv[rows] = dot(mix[onward, rows], pc[onward], TN)
-    save(pdk, pdk_out)
-    save(pdv, pdv_out)
 
     wait_bytes(yr.at[1, pl.ds(0, NY - 1)], y_recv.at[1])
 
@@ -334,6 +330,12 @@
     @pl.when(same_column)
     def _():
         fin[(x % 2) * NY + y] = zf[y]
+
+    for rows, upto, onward in blocks:
+        pdk[rows] = dot(gmix[onward, rows], pq[onward], TN)
+        pdv[rows] = dot(mix[onward, rows], pc[onward], TN)
+    save(pdk, pdk_out)
+    save(pdv, pdv_out)
 
     loads[6].wait()
     loads[7].wait()

time: 46.7 us -> 45 us (0.964)
  Pallas kernels: 44.6 us -> 42.9 us
    pallas_call x1, Pallas kernels: 41.2 us -> 39.5 us  [exchange(): pl.pallas_call(exchange_kernel, out_shape=tuple([jax.ShapeDtypeStruct((RO...]
where the time goes in v5:
time: 45 us; the launch traced here: 44.8 us
  Pallas kernels  42.9 us (95%)
  between operations  1.93 us (4%)
    pallas_call x1, Pallas kernels, exchange(): pl.pallas_call(exchange_kernel, out_shape=tuple([jax.ShapeDtypeStruct((RO...  39.5 us
    pallas_call x1, Pallas kernels, finish(): pl.pallas_call(finish_kernel, out_shape=tuple([jax.ShapeDtypeStruct((ROWS...  3.37 us

profile of v5, /device:TPU:1, one launch (start us, length us, event | category | flops | bytes accessed | tf_op | source)
XLA Modules:
  0.0 44.8 jit_solution(3509080080901544924)
XLA Ops:
  1.9 39.5 %exchange.1 = (bf16[1024,128]{1,0:T(8,128)(2,1)}, bf16[1024,128]{1,0:T(8,128)(2,1)}, bf16[1024,128]{1,0:T(8,128)(2,1)}, bf16[1024,128]{1,0:T(8,128)(2,1)}, bf16[...) custom-call(bf16[1024,128]{1,0:T(8,128)(2,1)} %bitcast.21, ...), custom_call_target="tpu_custom_call" | custom-call | tf_op jit(solution)/shard_map/exchange/pallas_call | solution.py:420
  41.5 3.4 %finish.1 = (bf16[1024,128]{1,0:T(8,128)(2,1)}, bf16[1024,128]{1,0:T(8,128)(2,1)}, bf16[1024,128]{1,0:T(8,128)(2,1)}, bf16[1024,128]{1,0:T(8,128)(2,1)}, bf16[10...) custom-call(bf16[1024,128]{1,0:T(8,128)(2,1)} %get-tuple-element.25.po_in, ...), custom_call_target="tpu_custom_call" | custom-call | tf_op jit(solution)/shard_map/finish/pallas_call | solution.py:501

commit v6 on v4

--- a/solution.py
+++ b/solution.py
@@ -251,8 +251,10 @@
               for i in range(ROWS // BLK)]
 
     mixings(pqs, pk, PROMPT_HEADS, mix)
-
-    for piece in range(NY // 2):
+    pcs[...] = scale_rows(pc[...], prompt_first, PROMPT_HEADS)
+    mixings(pcs, pv, PROMPT_HEADS, gmix)
+
+    for piece in range(3):
         y_piece(0, piece)
 
     wait_bytes(wy.at[pl.ds(0, NY - 1)], w_recv)
@@ -261,6 +263,7 @@
         send(wy.at[to], wq.at[z], v_send, v_recv, (y, x, 2 * to + c))
     wq[z] = wy[z]
 
+    y_piece(0, 3)
     for piece in range(NY // 2):
         y_piece(1, piece)
 
@@ -276,13 +279,10 @@
     def _(d):
         send(zf.at[z], zf.at[z], z_send, z_recv, (y, x, 2 * ((z + d) % NZ) + c))
 
-    pcs[...] = scale_rows(pc[...], prompt_first, PROMPT_HEADS)
-    mixings(pcs, pv, PROMPT_HEADS, gmix)
     for rows, upto, onward in blocks:
         part[0, rows] = dot(mix[rows, upto], pv[upto], NN)
         part[1, rows] = dot(gmix[rows, upto], pk[upto], NN)
 
-    s_piece(0, 0)
     wait_bytes(wq.at[pl.ds(0, NZ - 1)], v_recv)
     total = wq[0]
     for n in range(1, NZ):
@@ -296,10 +296,6 @@
     @pl.when(same_column)
     def _():
         wf[...] = wt[...]
-
-    s_piece(0, 1)
-    s_piece(0, 2)
-    s_piece(0, 3)
 
     for rows, upto, onward in blocks:
         pdk[rows] = dot(gmix[onward, rows], pq[onward], TN)
@@ -335,17 +331,22 @@
     def _():
         fin[(x % 2) * NY + y] = zf[y]
 
+    s_piece(0, 0)
+    s_piece(0, 1)
+    s_piece(0, 2)
+    s_piece(0, 3)
+
     loads[6].wait()
     loads[7].wait()
     mixings(rqs, rk, REPLY_HEADS, mix)
+    rcs[...] = scale_rows(rw[...], reply_first, REPLY_HEADS)
+    mixings(rcs, rv, REPLY_HEADS, gmix)
 
     s_piece(1, 0)
     s_piece(1, 1)
     s_piece(1, 2)
     s_piece(1, 3)
 
-    rcs[...] = scale_rows(rw[...], reply_first, REPLY_HEADS)
-    mixings(rcs, rv, REPLY_HEADS, gmix)
     for rows, upto, onward in blocks:
         rdv[rows] = dot(mix[onward, rows], rw[onward], TN).astype(BF16)
     save(rdv, rdv_out)
@@ -364,9 +365,6 @@
     pdq[...] = (part[1] + dot(by_head(pcs[...], PROMPT_HEADS), wide, NT)).astype(BF16)
     save(pdq, pdq_out)
 
-    collect(1, aft)
-    save(aft, aft_out)
-
     @pl.when(same_column)
     def _():
         wait_bytes(fin.at[pl.ds(0, 15)], f_recv)
@@ -383,6 +381,9 @@
     wide = stack_wide(final, REPLY_HEADS)
     rdq[...] = (part[3] + dot(by_head(rcs[...], REPLY_HEADS), wide, NT)).astype(BF16)
     save(rdq, rdq_out)
+
+    collect(1, aft)
+    save(aft, aft_out)
 
     for k in range(2):
         wait_bytes(loc.at[k, pl.ds(0, NX - 1)], x_send.at[k])

time: 46.7 us -> 45.3 us (0.970)
  Pallas kernels: 44.6 us -> 43.2 us
    pallas_call x1, Pallas kernels: 41.2 us -> 39.9 us  [exchange(): pl.pallas_call(exchange_kernel, out_shape=tuple([jax.ShapeDtypeStruct((RO...]
where the time goes in v6:
time: 45.3 us; the launch traced here: 45.2 us
  Pallas kernels  43.2 us (95%)
  between operations  1.93 us (4%)
    pallas_call x1, Pallas kernels, exchange(): pl.pallas_call(exchange_kernel, out_shape=tuple([jax.ShapeDtypeStruct((RO...  39.9 us
    pallas_call x1, Pallas kernels, finish(): pl.pallas_call(finish_kernel, out_shape=tuple([jax.ShapeDtypeStruct((ROWS...  3.37 us

profile of v6, /device:TPU:1, one launch (start us, length us, event | category | flops | bytes accessed | tf_op | source)
XLA Modules:
  0.0 45.2 jit_solution(13702413006782193921)
XLA Ops:
  1.9 39.9 %exchange.1 = (bf16[1024,128]{1,0:T(8,128)(2,1)}, bf16[1024,128]{1,0:T(8,128)(2,1)}, bf16[1024,128]{1,0:T(8,128)(2,1)}, bf16[1024,128]{1,0:T(8,128)(2,1)}, bf16[...) custom-call(bf16[1024,128]{1,0:T(8,128)(2,1)} %bitcast.21, ...), custom_call_target="tpu_custom_call" | custom-call | tf_op jit(solution)/shard_map/exchange/pallas_call | solution.py:419
  41.8 3.4 %finish.1 = (bf16[1024,128]{1,0:T(8,128)(2,1)}, bf16[1024,128]{1,0:T(8,128)(2,1)}, bf16[1024,128]{1,0:T(8,128)(2,1)}, bf16[1024,128]{1,0:T(8,128)(2,1)}, bf16[10...) custom-call(bf16[1024,128]{1,0:T(8,128)(2,1)} %get-tuple-element.25.po_in, ...), custom_call_target="tpu_custom_call" | custom-call | tf_op jit(solution)/shard_map/finish/pallas_call | solution.py:500

commit v7 on v6

--- a/solution.py
+++ b/solution.py
@@ -303,6 +303,11 @@
     save(pdk, pdk_out)
     save(pdv, pdv_out)
 
+    @pl.when(c == 1)
+    def _():
+        for piece in range(4):
+            s_piece(0, piece)
+
     wait_bytes(yr.at[1, pl.ds(0, NY - 1)], y_recv.at[1])
 
     @pl.when(jnp.logical_not(same_column))
@@ -331,10 +336,10 @@
     def _():
         fin[(x % 2) * NY + y] = zf[y]
 
-    s_piece(0, 0)
-    s_piece(0, 1)
-    s_piece(0, 2)
-    s_piece(0, 3)
+    @pl.when(c == 0)
+    def _():
+        for piece in range(4):
+            s_piece(0, piece)
 
     loads[6].wait()
     loads[7].wait()

time: 45.3 us -> 45.2 us (level)
  no operation moved by 1% of the time
where the time goes in v7:
time: 45.2 us; the launch traced here: 45.1 us
  Pallas kernels  43.1 us (95%)
  between operations  1.93 us (4%)
    pallas_call x1, Pallas kernels, exchange(): pl.pallas_call(exchange_kernel, out_shape=tuple([jax.ShapeDtypeStruct((RO...  39.8 us
    pallas_call x1, Pallas kernels, finish(): pl.pallas_call(finish_kernel, out_shape=tuple([jax.ShapeDtypeStruct((ROWS...  3.37 us

profile of v7, /device:TPU:1, one launch (start us, length us, event | category | flops | bytes accessed | tf_op | source)
XLA Modules:
  0.0 45.1 jit_solution(758158452799327971)
XLA Ops:
  1.9 39.8 %exchange.1 = (bf16[1024,128]{1,0:T(8,128)(2,1)}, bf16[1024,128]{1,0:T(8,128)(2,1)}, bf16[1024,128]{1,0:T(8,128)(2,1)}, bf16[1024,128]{1,0:T(8,128)(2,1)}, bf16[...) custom-call(bf16[1024,128]{1,0:T(8,128)(2,1)} %bitcast.21, ...), custom_call_target="tpu_custom_call" | custom-call | tf_op jit(solution)/shard_map/exchange/pallas_call | solution.py:424
  41.7 3.4 %finish.1 = (bf16[1024,128]{1,0:T(8,128)(2,1)}, bf16[1024,128]{1,0:T(8,128)(2,1)}, bf16[1024,128]{1,0:T(8,128)(2,1)}, bf16[1024,128]{1,0:T(8,128)(2,1)}, bf16[10...) custom-call(bf16[1024,128]{1,0:T(8,128)(2,1)} %get-tuple-element.25.po_in, ...), custom_call_target="tpu_custom_call" | custom-call | tf_op jit(solution)/shard_map/finish/pallas_call | solution.py:505
